TPU v7x, 1024 devices: a whole 8x8x8 slice. The times are simulated.
1024 devices in a mesh: dom: 128 (over y, z, core), sub: 8 (over x).
Axes of the slice: x: 8, y: 8, z: 8, core: 2. Of those that a mesh axis runs over, the one named last changes fastest.
Arguments:
- basis: float32 [2, 16, 1048576], P(None, None, ('dom', 'sub')), may hold values from -6 to 6
- compact: float32 [2, 32, 16], replicated, may hold values from -1 to 1
- weights: float32 [2, 2, 32], replicated, may hold values from -5 to 5
- fresh: float32 [2, 32], replicated, may hold values from -1 to 1
- shifts: float32 [2, 2], replicated, may hold values from -1 to 1
- k_tiles: float32 [8192, 3, 128, 128], P(('dom', 'sub'))
- pattern: int32 [8192, 2], P(('dom', 'sub')), may hold values from 0 to 63
- mass: float32 [1048576], P(('dom', 'sub')), may hold values from 0.5 to 2
- precond: float32 [8192, 2, 128, 128], P(('dom', 'sub'))
- c_tiles: float32 [8192, 128, 128], P(('dom', 'sub')), may hold values from -0.5 to 0.5
- c_rows: int32 [8192], P(('dom', 'sub')), may hold values from 0 to 7
- c_side: int32 [8192], P(('dom', 'sub')), may hold values from 0 to 1
- c_count: int32 [1024], P(('dom', 'sub')), may hold values from 1 to 8, as said below
Outputs:
- new_basis: float32 [2, 2, 1048576], P(None, None, ('dom', 'sub'))
- coeffs: float32 [2, 2, 18], replicated
Inputs may be any that keep to these rules, and one draw needn't show every extreme that they name: `pattern`: each tile row's coupled tiles lie in its own domain group. `c_rows`: a tile row of the device itself. `c_side`: 0 reads the domain below, 1 the domain above. The live slots of device d are its first c_count[d]; some device has all 8 live.
All inputs are finite; a program needn't handle non-finite values.
Results may differ from a plain program's by a relative error of at most 0.0003.
Values sent between devices are 32-bit elements; how exact they have to be, the bound alone decides.
A program may use at most 32 MiB of HBM per device.

v0:
```python
import jax
import jax.numpy as jnp
from jax import lax
from jax.sharding import Mesh
from jax.sharding import PartitionSpec as P

ITERS = 3
DOM_SUB = ("dom_0", "dom_1", "dom_2", "sub")
DOM = ("dom_0", "dom_1", "dom_2")


HIGH = lax.Precision.HIGHEST
EPSILON = 1e-06


def one_axis_at_a_time(array, axes):
    for axis in axes:
        array = lax.psum(array, axis)
    return array


def from_everyone(array, axis):
    copies = jnp.broadcast_to(array, (lax.axis_size(axis), *array.shape))
    return lax.all_to_all(copies, axis, split_axis=0, concat_axis=0, tiled=True)


def of_everyone(array, axis):
    return from_everyone(array, axis).sum(axis=0)


def in_one(arrays, axis):
    flat, at, done = (jnp.concatenate([a.reshape(-1) for a in arrays]), 0, [])
    so_far = of_everyone(flat, axis)
    for a in arrays:
        done.append(so_far[at : at + a.size].reshape(a.shape))
        at += a.size
    return tuple(done)


def in_order(tiles, dim):
    tiles = jnp.moveaxis(tiles, 0, dim)
    dims = tiles.shape
    return tiles.reshape(*dims[:dim], dims[dim] * dims[dim + 1], *dims[dim + 2 :])


def gathered_copies(array, axis, dim):
    tiles = from_everyone(array, axis)
    return in_order(tiles, dim)


def with_halo(cells, sides, width):
    for axis, dim in sides:
        count = lax.axis_size(axis)
        ends = count - 1
        head = lax.slice_in_dim(cells, 0, width, axis=dim)
        tail = lax.slice_in_dim(cells, cells.shape[dim] - width, cells.shape[dim], axis=dim)
        cells = jnp.concatenate(
            [
                lax.ppermute(tail, axis, [(i, (i + 1) % count) for i in range(ends)]),
                cells,
                lax.ppermute(head, axis, [((i + 1) % count, i) for i in range(ends)]),
            ],
            axis=dim,
        )
    return cells


def solve_normal(matrix, vector):
    order = vector.shape[0]
    lower = [[None] * order for number in range(order)]
    for target in range(order):
        for source in range(target + 1):
            value = matrix[target, source]
            for middle in range(source):
                value = value - lower[target][middle] * lower[source][middle]
            if target == source:
                lower[target][target] = jnp.sqrt(value)
            else:
                lower[target][source] = value / lower[source][source]
    forward = []
    for target in range(order):
        value = vector[target]
        for middle in range(target):
            value = value - lower[target][middle] * forward[middle]
        forward.append(value / lower[target][target])
    result = [None] * order
    for target in reversed(range(order)):
        value = forward[target]
        for middle in range(target + 1, order):
            value = value - lower[middle][target] * result[middle]
        result[target] = value / lower[target][target]
    return jnp.stack(result)


def combine(coef_real, coef_imag, stack):
    real = jnp.dot(coef_real, stack[0], precision=HIGH) - jnp.dot(
        coef_imag, stack[1], precision=HIGH
    )
    imag = jnp.dot(coef_real, stack[1], precision=HIGH) + jnp.dot(
        coef_imag, stack[0], precision=HIGH
    )
    return jnp.stack([real, imag])


def conj_products(stack, vector):
    real = jnp.dot(stack[0], vector[0], precision=HIGH) + jnp.dot(
        stack[1], vector[1], precision=HIGH
    )
    imag = jnp.dot(stack[0], vector[1], precision=HIGH) - jnp.dot(
        stack[1], vector[0], precision=HIGH
    )
    return (real, imag)


def precondition(vector, precond):
    count, tile = (precond.shape[0], precond.shape[2])
    blocks = vector.reshape(2, count, tile)
    real = jnp.einsum("tij,tj->ti", precond[:, 0], blocks[0], precision=HIGH) - jnp.einsum(
        "tij,tj->ti", precond[:, 1], blocks[1], precision=HIGH
    )
    imag = jnp.einsum("tij,tj->ti", precond[:, 0], blocks[1], precision=HIGH) + jnp.einsum(
        "tij,tj->ti", precond[:, 1], blocks[0], precision=HIGH
    )
    return jnp.stack([real, imag]).reshape(2, -1)


def apply_shift(stiff, vector, mass, shift_pair):
    moved_real = mass * vector[0]
    moved_imag = mass * vector[1]
    real = stiff[0] - (shift_pair[0] * moved_real - shift_pair[1] * moved_imag)
    imag = stiff[1] - (shift_pair[0] * moved_imag + shift_pair[1] * moved_real)
    return jnp.stack([real, imag])


def gram_parts(stack):
    real = jnp.dot(stack[0], stack[0].T, precision=HIGH) + jnp.dot(
        stack[1], stack[1].T, precision=HIGH
    )
    imag = jnp.dot(stack[0], stack[1].T, precision=HIGH) - jnp.dot(
        stack[1], stack[0].T, precision=HIGH
    )
    return (real, imag)


def minimal_coefficients(gram_real, gram_imag, order):
    top = jnp.concatenate([gram_real[:order, :order], -gram_imag[:order, :order]], axis=1)
    bottom = jnp.concatenate([gram_imag[:order, :order], gram_real[:order, :order]], axis=1)
    system = jnp.concatenate([top, bottom], axis=0)
    target = jnp.concatenate([gram_real[:order, order], gram_imag[:order, order]])
    solved = solve_normal(system, target)
    return (solved[:order], solved[order:])


def gram_total(gram_real, gram_imag):
    return (one_axis_at_a_time(gram_real, DOM_SUB), one_axis_at_a_time(gram_imag, DOM_SUB))


def project_total(proj_real, proj_imag):
    inside = in_one((proj_real, proj_imag), "sub")
    return (one_axis_at_a_time(inside[0], DOM), one_axis_at_a_time(inside[1], DOM))


def square_total(value):
    inside = of_everyone(value, "sub")
    return one_axis_at_a_time(inside, DOM)


def local(
    basis,
    compact,
    weights,
    fresh,
    shifts,
    k_tiles,
    pattern,
    mass,
    precond,
    c_tiles,
    c_rows,
    c_side,
    c_count,
):
    tiles_dev = k_tiles.shape[0]
    tile = k_tiles.shape[2]
    rows_dev = tiles_dev * tile
    total_rows = rows_dev * lax.axis_size(DOM) * lax.axis_size("sub")
    ownrow = lax.axis_index("sub") * tiles_dev + jnp.arange(tiles_dev, dtype=jnp.int32)
    columns = jnp.concatenate([ownrow[:, None], pattern], axis=1)
    slot_count = c_tiles.shape[0]
    live_mask = (jnp.arange(slot_count, dtype=jnp.int32) < c_count[0]).astype(jnp.float32)
    previous = jnp.zeros((2, rows_dev), jnp.float32)
    made = []
    listed = []
    for step in range(weights.shape[0]):
        beta_real = weights[step, 0]
        beta_imag = weights[step, 1]
        coef_real = jnp.dot(beta_real, compact[0], precision=HIGH) - jnp.dot(
            beta_imag, compact[1], precision=HIGH
        )
        coef_imag = jnp.dot(beta_real, compact[1], precision=HIGH) + jnp.dot(
            beta_imag, compact[0], precision=HIGH
        )
        gamma_real = jnp.sum(beta_real * fresh[0] - beta_imag * fresh[1])
        gamma_imag = jnp.sum(beta_real * fresh[1] + beta_imag * fresh[0])
        extended = jnp.concatenate([basis, previous[:, None, :]], axis=1)
        right = combine(
            jnp.concatenate([coef_real, gamma_real[None]]),
            jnp.concatenate([coef_imag, gamma_imag[None]]),
            extended,
        )
        terms = [right]
        images = []
        for index in range(ITERS):
            vector = precondition(terms[-1], precond)
            whole = gathered_copies(vector, "sub", 1)
            blocks = whole.reshape(2, -1, tile)
            stiff = jnp.einsum("tsij,ctsj->cti", k_tiles, blocks[:, columns], precision=HIGH)
            result = apply_shift(stiff.reshape(2, rows_dev), vector, mass, shifts[step])
            padded = with_halo(vector, ((DOM, 1),), tile)
            rims = jnp.stack([padded[:, :tile], padded[:, padded.shape[1] - tile :]], axis=1)
            sources = rims[:, c_side]
            contrib = (
                jnp.einsum("sij,csj->csi", c_tiles, sources, precision=HIGH)
                * live_mask[None, :, None]
            )
            onehot = (c_rows[:, None] == jnp.arange(tiles_dev, dtype=jnp.int32)[None, :]).astype(
                jnp.float32
            )
            extra = jnp.einsum("csi,st->cti", contrib, onehot, precision=HIGH)
            image = result + extra.reshape(2, rows_dev)
            images.append(image)
            if index + 1 < ITERS:
                terms.append(image - terms[-1])
        stacked = jnp.stack(images + [right], axis=1)
        local_real, local_imag = gram_parts(stacked)
        gram_real, gram_imag = gram_total(local_real, local_imag)
        solve_real, solve_imag = minimal_coefficients(gram_real, gram_imag, ITERS)
        direction = combine(solve_real, solve_imag, jnp.stack(terms, axis=1))
        solution = precondition(direction, precond)
        part_real, part_imag = conj_products(extended, solution)
        proj_real, proj_imag = project_total(part_real, part_imag)
        proj_real = proj_real / total_rows
        proj_imag = proj_imag / total_rows
        remain = solution - combine(proj_real, proj_imag, extended)
        squares = square_total(jnp.sum(remain * remain))
        norm = jnp.sqrt(squares / total_rows + EPSILON)
        latest = remain / norm
        made.append(latest)
        listed.append(
            jnp.stack(
                [
                    jnp.concatenate([proj_real, norm[None]]),
                    jnp.concatenate([proj_imag, jnp.zeros((1,), jnp.float32)]),
                ]
            )
        )
        previous = latest
    return (jnp.stack(made), jnp.stack(listed))


def solution(mesh):
    torus = Mesh(
        mesh.devices.reshape(8, 8, 2, mesh.shape["sub"]), ("dom_0", "dom_1", "dom_2", "sub")
    )
    placed = (
        P(None, None, DOM_SUB),
        P(),
        P(),
        P(),
        P(),
        P(DOM_SUB, None, None, None),
        P(DOM_SUB, None),
        P(DOM_SUB),
        P(DOM_SUB, None, None, None),
        P(DOM_SUB, None, None),
        P(DOM_SUB),
        P(DOM_SUB),
        P(DOM_SUB),
    )
    return jax.shard_map(
        local, mesh=torus, in_specs=placed, out_specs=(P(None, None, DOM_SUB), P()), check_vma=False
    )
```

profile of v0, /device:TPU:1, one launch (start us, length us, event | category | flops | bytes accessed | tf_op | source)
XLA Modules:
  0.0 541.0 jit_solution(14922405235763412547)
XLA Ops:
  18.4 6.3 %collective-permute-start = (f32[2,128]{1,0:T(2,128)S(1)}, f32[2,128]{1,0:T(2,128)S(1)}, u32[]{:S(2)}, u32[]{:S(2)}) collective-permute-start(f32[2,128]{1,0:T(2,128)S(1)} %get-tuple-element.90), channel_id=1, source_target_pairs={{0,8},{8,16},{16,24},{24,32},{32,40},{40,48},{48,56},{56,64},{64,7... | collective-permute-start | bytes 3080 | tf_op jit(solution)/shard_map/ppermute | solution.py:59
  24.7 11.0 %collective-permute-start.1 = (f32[2,128]{1,0:T(2,128)S(1)}, f32[2,128]{1,0:T(2,128)S(1)}, u32[]{:S(2)}, u32[]{:S(2)}) collective-permute-start(f32[2,128]{1,0:T(2,128)S(1)} %get-tuple-element.91), channel_id=1, source_target_pairs={{8,0},{16,8},{24,16},{32,24},{40,32},{48,40},{56,48},{64,56},{72,6... | collective-permute-start | bytes 3080 | tf_op jit(solution)/shard_map/ppermute | solution.py:61
  65.4 6.3 %all-to-all-done.1 = f32[8,2,1024]{2,1,0:T(2,128)S(1)} async-done(((f32[8,2,1024]{2,1,0:T(2,128)}), f32[8,2,1024]{2,1,0:T(2,128)S(1)}, u32[]{:S(2)}, u32[]{:S(2)}) %all-to-all-start.1) | async-done | bytes 65568 | tf_op jit(solution)/shard_map/all_to_all | solution.py:24
  90.3 5.5 %all-to-all-done.2 = f32[8,2,1024]{2,1,0:T(2,128)S(1)} async-done(((f32[8,2,1024]{2,1,0:T(2,128)}), f32[8,2,1024]{2,1,0:T(2,128)S(1)}, u32[]{:S(2)}, u32[]{:S(2)}) %all-to-all-start.2) | async-done | bytes 65568 | tf_op jit(solution)/shard_map/all_to_all | solution.py:24
  100.3 24.1 %all-reduce.10 = (f32[4,4]{1,0:T(4,128)S(1)}, f32[4,4]{1,0:T(4,128)S(1)}) all-reduce(f32[4,4]{1,0:T(4,128)S(1)} %convolution_add_fusion.1, f32[4,4]{1,0:T(4,128)S(1)} %convolution_subtract_fusion.1), channel_id=1, replica_groups=mesh['dom_0'=8,'dom_1'=8,'dom_2'=2,'sub'=8] {'dom_0'}, use_global_device_ids=true, to_apply=%region_2.0 | all-reduce | flops 32 | bytes 256 | tf_op jit(solution)/shard_map/psum | solution.py:18
  124.3 13.4 %all-reduce.6 = (f32[4,4]{1,0:T(4,128)S(1)}, f32[4,4]{1,0:T(4,128)S(1)}) all-reduce(f32[4,4]{1,0:T(4,128)S(1)} %get-tuple-element.24, f32[4,4]{1,0:T(4,128)S(1)} %get-tuple-element.25), channel_id=1, replica_groups=mesh['dom_0'=8,'dom_1'=8,'dom_2'=2,'sub'=8] {'dom_1'}, use_global_device_ids=true, to_apply=%region_3.0 | all-reduce | flops 32 | bytes 256 | tf_op jit(solution)/shard_map/psum | solution.py:18
  137.8 11.6 %all-reduce.14 = (f32[4,4]{1,0:T(4,128)S(1)}, f32[4,4]{1,0:T(4,128)S(1)}) all-reduce(f32[4,4]{1,0:T(4,128)S(1)} %get-tuple-element.16, f32[4,4]{1,0:T(4,128)S(1)} %get-tuple-element.17), channel_id=1, replica_groups=mesh['dom_0'=8,'dom_1'=8,'dom_2'=2,'sub'=8] {'dom_2'}, use_global_device_ids=true, to_apply=%region_4.0 | all-reduce | flops 32 | bytes 256 | tf_op jit(solution)/shard_map/psum | solution.py:18
  149.3 10.9 %all-reduce.2 = (f32[4,4]{1,0:T(4,128)S(1)}, f32[4,4]{1,0:T(4,128)S(1)}) all-reduce(f32[4,4]{1,0:T(4,128)S(1)} %get-tuple-element.32, f32[4,4]{1,0:T(4,128)S(1)} %get-tuple-element.33), channel_id=1, replica_groups=mesh['dom_0'=8,'dom_1'=8,'dom_2'=2,'sub'=8] {'sub'}, use_global_device_ids=true, to_apply=%region_5.0 | all-reduce | flops 32 | bytes 256 | tf_op jit(solution)/shard_map/psum | solution.py:18
  189.5 6.4 %all-to-all-done.3 = f32[8,1,34]{2,1,0:T(1,128)S(1)} async-done(((f32[8,1,34]{2,1,0:T(1,128)}), f32[8,1,34]{2,1,0:T(1,128)S(1)}, u32[]{:S(2)}, u32[]{:S(2)}) %all-to-all-start.3) | async-done | bytes 1120 | tf_op jit(solution)/shard_map/all_to_all | solution.py:24
  196.0 12.5 %all-reduce.9 = (f32[17]{0:T(128)S(1)}, f32[17]{0:T(128)S(1)}) all-reduce(f32[17]{0:T(128)S(1)} %get-tuple-element.141, f32[17]{0:T(128)S(1)} %get-tuple-element.140), channel_id=1, replica_groups=mesh['dom_0'=8,'dom_1'=8,'dom_2'=2,'sub'=8] {'dom_0'}, use_global_device_ids=true, to_apply=%region_11.0 | all-reduce | flops 34 | bytes 272 | tf_op jit(solution)/shard_map/psum | solution.py:18
  208.4 12.6 %all-reduce.5 = (f32[17]{0:T(128)S(1)}, f32[17]{0:T(128)S(1)}) all-reduce(f32[17]{0:T(128)S(1)} %get-tuple-element.22, f32[17]{0:T(128)S(1)} %get-tuple-element.23), channel_id=1, replica_groups=mesh['dom_0'=8,'dom_1'=8,'dom_2'=2,'sub'=8] {'dom_1'}, use_global_device_ids=true, to_apply=%region_12.0 | all-reduce | flops 34 | bytes 272 | tf_op jit(solution)/shard_map/psum | solution.py:18
  221.0 14.8 %all-reduce.13 = (f32[17]{0:T(128)S(1)}, f32[17]{0:T(128)S(1)}) all-reduce(f32[17]{0:T(128)S(1)} %get-tuple-element.14, f32[17]{0:T(128)S(1)} %get-tuple-element.15), channel_id=1, replica_groups=mesh['dom_0'=8,'dom_1'=8,'dom_2'=2,'sub'=8] {'dom_2'}, use_global_device_ids=true, to_apply=%region_13.0 | all-reduce | flops 34 | bytes 272 | tf_op jit(solution)/shard_map/psum | solution.py:18
  242.1 6.3 %all-to-all-done.4 = f32[8,1,1]{2,1,0:T(1,128)S(1)} async-done(((f32[8,1,1]{2,1,0:T(1,128)}), f32[8,1,1]{2,1,0:T(1,128)S(1)}, u32[]{:S(2)}, u32[]{:S(2)}) %all-to-all-start.4) | async-done | bytes 64 | tf_op jit(solution)/shard_map/all_to_all | solution.py:24
  249.0 11.3 %psum.252 = f32[]{:T(128)} all-reduce(f32[]{:T(128)} %reduce_sum.94), channel_id=1, replica_groups=mesh['dom_0'=8,'dom_1'=8,'dom_2'=2,'sub'=8] {'dom_0'}, use_global_device_ids=true, to_apply=%region_19.0 | all-reduce | flops 1 | bytes 8 | tf_op jit(solution)/shard_map/psum | solution.py:18
  260.3 11.4 %psum.253 = f32[]{:T(128)} all-reduce(f32[]{:T(128)} %psum.252), channel_id=1, replica_groups=mesh['dom_0'=8,'dom_1'=8,'dom_2'=2,'sub'=8] {'dom_1'}, use_global_device_ids=true, to_apply=%region_20.0 | all-reduce | flops 1 | bytes 8 | tf_op jit(solution)/shard_map/psum | solution.py:18
  271.8 11.1 %psum.254 = f32[]{:T(128)} all-reduce(f32[]{:T(128)} %psum.253), channel_id=1, replica_groups=mesh['dom_0'=8,'dom_1'=8,'dom_2'=2,'sub'=8] {'dom_2'}, use_global_device_ids=true, to_apply=%region_21.0 | all-reduce | flops 1 | bytes 8 | tf_op jit(solution)/shard_map/psum | solution.py:18
  302.5 5.5 %all-to-all-done.5 = f32[8,2,1024]{2,1,0:T(2,128)S(1)} async-done(((f32[8,2,1024]{2,1,0:T(2,128)}), f32[8,2,1024]{2,1,0:T(2,128)S(1)}, u32[]{:S(2)}, u32[]{:S(2)}) %all-to-all-start.5) | async-done | bytes 65568 | tf_op jit(solution)/shard_map/all_to_all | solution.py:24
  315.5 4.8 collective-permute-start.8
  328.1 5.5 %all-to-all-done.6 = f32[8,2,1024]{2,1,0:T(2,128)S(1)} async-done(((f32[8,2,1024]{2,1,0:T(2,128)}), f32[8,2,1024]{2,1,0:T(2,128)S(1)}, u32[]{:S(2)}, u32[]{:S(2)}) %all-to-all-start.6) | async-done | bytes 65568 | tf_op jit(solution)/shard_map/all_to_all | solution.py:24
  353.5 5.5 %all-to-all-done.7 = f32[8,2,1024]{2,1,0:T(2,128)S(1)} async-done(((f32[8,2,1024]{2,1,0:T(2,128)}), f32[8,2,1024]{2,1,0:T(2,128)S(1)}, u32[]{:S(2)}, u32[]{:S(2)}) %all-to-all-start.7) | async-done | bytes 65568 | tf_op jit(solution)/shard_map/all_to_all | solution.py:24
  363.5 15.0 %all-reduce.8 = (f32[4,4]{1,0:T(4,128)S(1)}, f32[4,4]{1,0:T(4,128)S(1)}) all-reduce(f32[4,4]{1,0:T(4,128)S(1)} %convolution_add_fusion, f32[4,4]{1,0:T(4,128)S(1)} %convolution_subtract_fusion), channel_id=1, replica_groups=mesh['dom_0'=8,'dom_1'=8,'dom_2'=2,'sub'=8] {'dom_0'}, use_global_device_ids=true, to_apply=%region_24.0 | all-reduce | flops 32 | bytes 256 | tf_op jit(solution)/shard_map/psum | solution.py:18
  378.5 15.1 %all-reduce.4 = (f32[4,4]{1,0:T(4,128)S(1)}, f32[4,4]{1,0:T(4,128)S(1)}) all-reduce(f32[4,4]{1,0:T(4,128)S(1)} %get-tuple-element.20, f32[4,4]{1,0:T(4,128)S(1)} %get-tuple-element.21), channel_id=1, replica_groups=mesh['dom_0'=8,'dom_1'=8,'dom_2'=2,'sub'=8] {'dom_1'}, use_global_device_ids=true, to_apply=%region_25.0 | all-reduce | flops 32 | bytes 256 | tf_op jit(solution)/shard_map/psum | solution.py:18
  393.6 10.3 %all-reduce.12 = (f32[4,4]{1,0:T(4,128)S(1)}, f32[4,4]{1,0:T(4,128)S(1)}) all-reduce(f32[4,4]{1,0:T(4,128)S(1)} %get-tuple-element.12, f32[4,4]{1,0:T(4,128)S(1)} %get-tuple-element.13), channel_id=1, replica_groups=mesh['dom_0'=8,'dom_1'=8,'dom_2'=2,'sub'=8] {'dom_2'}, use_global_device_ids=true, to_apply=%region_26.0 | all-reduce | flops 32 | bytes 256 | tf_op jit(solution)/shard_map/psum | solution.py:18
  403.9 10.9 %all-reduce.1 = (f32[4,4]{1,0:T(4,128)S(1)}, f32[4,4]{1,0:T(4,128)S(1)}) all-reduce(f32[4,4]{1,0:T(4,128)S(1)} %get-tuple-element.28, f32[4,4]{1,0:T(4,128)S(1)} %get-tuple-element.29), channel_id=1, replica_groups=mesh['dom_0'=8,'dom_1'=8,'dom_2'=2,'sub'=8] {'sub'}, use_global_device_ids=true, to_apply=%region_27.0 | all-reduce | flops 32 | bytes 256 | tf_op jit(solution)/shard_map/psum | solution.py:18
  444.2 6.4 %all-to-all-done.8 = f32[8,1,34]{2,1,0:T(1,128)S(1)} async-done(((f32[8,1,34]{2,1,0:T(1,128)}), f32[8,1,34]{2,1,0:T(1,128)S(1)}, u32[]{:S(2)}, u32[]{:S(2)}) %all-to-all-start.8) | async-done | bytes 1120 | tf_op jit(solution)/shard_map/all_to_all | solution.py:24
  450.7 13.7 %all-reduce.7 = (f32[17]{0:T(128)S(1)}, f32[17]{0:T(128)S(1)}) all-reduce(f32[17]{0:T(128)S(1)} %get-tuple-element.139, f32[17]{0:T(128)S(1)} %get-tuple-element.138), channel_id=1, replica_groups=mesh['dom_0'=8,'dom_1'=8,'dom_2'=2,'sub'=8] {'dom_0'}, use_global_device_ids=true, to_apply=%region_33.0 | all-reduce | flops 34 | bytes 272 | tf_op jit(solution)/shard_map/psum | solution.py:18
  464.4 12.4 %all-reduce.3 = (f32[17]{0:T(128)S(1)}, f32[17]{0:T(128)S(1)}) all-reduce(f32[17]{0:T(128)S(1)} %get-tuple-element.18, f32[17]{0:T(128)S(1)} %get-tuple-element.19), channel_id=1, replica_groups=mesh['dom_0'=8,'dom_1'=8,'dom_2'=2,'sub'=8] {'dom_1'}, use_global_device_ids=true, to_apply=%region_34.0 | all-reduce | flops 34 | bytes 272 | tf_op jit(solution)/shard_map/psum | solution.py:18
  476.7 15.1 %all-reduce.11 = (f32[17]{0:T(128)S(1)}, f32[17]{0:T(128)S(1)}) all-reduce(f32[17]{0:T(128)S(1)} %get-tuple-element.10, f32[17]{0:T(128)S(1)} %get-tuple-element.11), channel_id=1, replica_groups=mesh['dom_0'=8,'dom_1'=8,'dom_2'=2,'sub'=8] {'dom_2'}, use_global_device_ids=true, to_apply=%region_35.0 | all-reduce | flops 34 | bytes 272 | tf_op jit(solution)/shard_map/psum | solution.py:18
  497.7 6.4 %all-to-all-done.9 = f32[8,1,1]{2,1,0:T(1,128)S(1)} async-done(((f32[8,1,1]{2,1,0:T(1,128)}), f32[8,1,1]{2,1,0:T(1,128)S(1)}, u32[]{:S(2)}, u32[]{:S(2)}) %all-to-all-start.9) | async-done | bytes 64 | tf_op jit(solution)/shard_map/all_to_all | solution.py:24
  504.7 11.3 %psum.269 = f32[]{:T(128)} all-reduce(f32[]{:T(128)} %reduce_sum.99), channel_id=1, replica_groups=mesh['dom_0'=8,'dom_1'=8,'dom_2'=2,'sub'=8] {'dom_0'}, use_global_device_ids=true, to_apply=%region_41.0 | all-reduce | flops 1 | bytes 8 | tf_op jit(solution)/shard_map/psum | solution.py:18
  516.0 11.4 %psum.270 = f32[]{:T(128)} all-reduce(f32[]{:T(128)} %psum.269), channel_id=1, replica_groups=mesh['dom_0'=8,'dom_1'=8,'dom_2'=2,'sub'=8] {'dom_1'}, use_global_device_ids=true, to_apply=%region_42.0 | all-reduce | flops 1 | bytes 8 | tf_op jit(solution)/shard_map/psum | solution.py:18
  527.4 11.1 %psum.271 = f32[]{:T(128)} all-reduce(f32[]{:T(128)} %psum.270), channel_id=1, replica_groups=mesh['dom_0'=8,'dom_1'=8,'dom_2'=2,'sub'=8] {'dom_2'}, use_global_device_ids=true, to_apply=%region_43.0 | all-reduce | flops 1 | bytes 8 | tf_op jit(solution)/shard_map/psum | solution.py:18
  (293 shorter events, 165.1 us)
Async XLA Ops:
  0.6 47.7 %copy-start = (f32[8,3,128,128]{3,2,1,0:T(8,128)S(1)}, f32[8,3,128,128]{3,2,1,0:T(8,128)}, u32[]{:S(2)}) copy-start(f32[8,3,128,128]{3,2,1,0:T(8,128)} %param.18) | copy-start | bytes 4718596
  0.6 39.1 %copy-start.6 = (f32[2,2,32]{2,1,0:T(2,128)S(1)}, f32[2,2,32]{2,1,0:T(2,128)}, u32[]{:S(2)}) copy-start(f32[2,2,32]{2,1,0:T(2,128)} %param.15) | copy-start | bytes 1540
  0.7 39.1 %copy-start.4 = (f32[2,32,16]{1,2,0:T(8,128)S(1)}, f32[2,32,16]{1,2,0:T(8,128)}, u32[]{:S(2)}) copy-start(f32[2,32,16]{1,2,0:T(8,128)} %param.14) | copy-start | bytes 12292
  0.7 39.9 %copy-start.10 = (s32[8]{0:T(128)S(1)}, s32[8]{0:T(128)}, u32[]{:S(2)}) copy-start(s32[8]{0:T(128)} %param.24) | copy-start | bytes 100
  0.7 40.1 %copy-start.9 = (s32[8,2]{0,1:T(2,128)S(1)}, s32[8,2]{0,1:T(2,128)}, u32[]{:S(2)}) copy-start(s32[8,2]{0,1:T(2,128)} %param.19) | copy-start | bytes 196
  0.7 40.2 %copy-start.8 = (f32[2,2]{1,0:T(2,128)S(1)}, f32[2,2]{1,0:T(2,128)}, u32[]{:S(2)}) copy-start(f32[2,2]{1,0:T(2,128)} %param.17) | copy-start | bytes 52
  0.7 41.5 %copy-start.3 = (f32[8,128,128]{2,1,0:T(8,128)S(1)}, f32[8,128,128]{2,1,0:T(8,128)}, u32[]{:S(2)}) copy-start(f32[8,128,128]{2,1,0:T(8,128)} %param.22) | copy-start | bytes 1572868
  10.8 32.3 %copy-start.7 = (s32[8]{0:T(128)S(1)}, s32[8]{0:T(128)}, u32[]{:S(2)}) copy-start(s32[8]{0:T(128)} %param.23) | copy-start | bytes 100
  17.5 32.7 %copy-start.5 = (f32[1024]{0:T(1024)S(1)}, f32[1024]{0:T(1024)}, u32[]{:S(2)}) copy-start(f32[1024]{0:T(1024)} %param.20) | copy-start | bytes 12292
  18.4 23.2 %collective-permute-start = (f32[2,128]{1,0:T(2,128)S(1)}, f32[2,128]{1,0:T(2,128)S(1)}, u32[]{:S(2)}, u32[]{:S(2)}) collective-permute-start(f32[2,128]{1,0:T(2,128)S(1)} %get-tuple-element.90), channel_id=1, source_target_pairs={{0,8},{8,16},{16,24},{24,32},{32,40},{40,48},{48,56},{56,64},{64,7... | collective-permute-start | bytes 3080 | tf_op jit(solution)/shard_map/ppermute | solution.py:59
  24.7 16.9 %collective-permute-start.1 = (f32[2,128]{1,0:T(2,128)S(1)}, f32[2,128]{1,0:T(2,128)S(1)}, u32[]{:S(2)}, u32[]{:S(2)}) collective-permute-start(f32[2,128]{1,0:T(2,128)S(1)} %get-tuple-element.91), channel_id=1, source_target_pairs={{8,0},{16,8},{24,16},{32,24},{40,32},{48,40},{56,48},{64,56},{72,6... | collective-permute-start | bytes 3080 | tf_op jit(solution)/shard_map/ppermute | solution.py:61
  36.4 11.3 %all-to-all-start = ((f32[8,2,1024]{2,1,0:T(2,128)}), f32[8,2,1024]{2,1,0:T(2,128)S(1)}, u32[]{:S(2)}, u32[]{:S(2)}) async-start(f32[8,2,1024]{2,1,0:T(2,128)} %broadcast_in_dim.36), calls=%async_computation | async-start | bytes 131072 | tf_op jit(solution)/shard_map/all_to_all | solution.py:24
  55.2 8.5 %collective-permute-start.2 = (f32[2,128]{1,0:T(2,128)S(1)}, f32[2,128]{1,0:T(2,128)S(1)}, u32[]{:S(2)}, u32[]{:S(2)}) collective-permute-start(f32[2,128]{1,0:T(2,128)S(1)} %get-tuple-element.86), channel_id=1, source_target_pairs={{0,8},{8,16},{16,24},{24,32},{32,40},{40,48},{48,56},{56,64},{64,7... | collective-permute-start | bytes 3080 | tf_op jit(solution)/shard_map/ppermute | solution.py:59
  57.2 6.6 %collective-permute-start.3 = (f32[2,128]{1,0:T(2,128)S(1)}, f32[2,128]{1,0:T(2,128)S(1)}, u32[]{:S(2)}, u32[]{:S(2)}) collective-permute-start(f32[2,128]{1,0:T(2,128)S(1)} %get-tuple-element.87), channel_id=1, source_target_pairs={{8,0},{16,8},{24,16},{32,24},{40,32},{48,40},{56,48},{64,56},{72,6... | collective-permute-start | bytes 3080 | tf_op jit(solution)/shard_map/ppermute | solution.py:61
  60.2 11.5 %all-to-all-start.1 = ((f32[8,2,1024]{2,1,0:T(2,128)}), f32[8,2,1024]{2,1,0:T(2,128)S(1)}, u32[]{:S(2)}, u32[]{:S(2)}) async-start(f32[8,2,1024]{2,1,0:T(2,128)} %broadcast_in_dim.38), calls=%async_computation.1 | async-start | bytes 131072 | tf_op jit(solution)/shard_map/all_to_all | solution.py:24
  79.2 9.4 %collective-permute-start.4 = (f32[2,128]{1,0:T(2,128)S(1)}, f32[2,128]{1,0:T(2,128)S(1)}, u32[]{:S(2)}, u32[]{:S(2)}) collective-permute-start(f32[2,128]{1,0:T(2,128)S(1)} %get-tuple-element.80), channel_id=1, source_target_pairs={{0,8},{8,16},{16,24},{24,32},{32,40},{40,48},{48,56},{56,64},{64,7... | collective-permute-start | bytes 3080 | tf_op jit(solution)/shard_map/ppermute | solution.py:59
  82.7 6.0 %collective-permute-start.5 = (f32[2,128]{1,0:T(2,128)S(1)}, f32[2,128]{1,0:T(2,128)S(1)}, u32[]{:S(2)}, u32[]{:S(2)}) collective-permute-start(f32[2,128]{1,0:T(2,128)S(1)} %get-tuple-element.81), channel_id=1, source_target_pairs={{8,0},{16,8},{24,16},{32,24},{40,32},{48,40},{56,48},{64,56},{72,6... | collective-permute-start | bytes 3080 | tf_op jit(solution)/shard_map/ppermute | solution.py:61
  85.2 10.5 %all-to-all-start.2 = ((f32[8,2,1024]{2,1,0:T(2,128)}), f32[8,2,1024]{2,1,0:T(2,128)S(1)}, u32[]{:S(2)}, u32[]{:S(2)}) async-start(f32[8,2,1024]{2,1,0:T(2,128)} %broadcast_in_dim.39), calls=%async_computation.2 | async-start | bytes 131072 | tf_op jit(solution)/shard_map/all_to_all | solution.py:24
  99.4 85.0 %copy-start.2 = (f32[2,16,1024]{2,1,0:T(8,128)S(1)}, f32[2,16,1024]{2,1,0:T(8,128)}, u32[]{:S(2)}) copy-start(f32[2,16,1024]{2,1,0:T(8,128)} %param.13) | copy-start | bytes 393220
  185.9 10.0 %all-to-all-start.3 = ((f32[8,1,34]{2,1,0:T(1,128)}), f32[8,1,34]{2,1,0:T(1,128)S(1)}, u32[]{:S(2)}, u32[]{:S(2)}) async-start(f32[8,1,34]{2,1,0:T(1,128)} %broadcast_in_dim.40), calls=%async_computation.3 | async-start | bytes 8192 | tf_op jit(solution)/shard_map/all_to_all | solution.py:24
  238.5 9.9 %all-to-all-start.4 = ((f32[8,1,1]{2,1,0:T(1,128)}), f32[8,1,1]{2,1,0:T(1,128)S(1)}, u32[]{:S(2)}, u32[]{:S(2)}) async-start(f32[8,1,1]{2,1,0:T(1,128)} %broadcast_in_dim.41), calls=%async_computation.4 | async-start | bytes 8192 | tf_op jit(solution)/shard_map/all_to_all | solution.py:24
  291.0 9.8 %collective-permute-start.6 = (f32[2,128]{1,0:T(2,128)S(1)}, f32[2,128]{1,0:T(2,128)S(1)}, u32[]{:S(2)}, u32[]{:S(2)}) collective-permute-start(f32[2,128]{1,0:T(2,128)S(1)} %get-tuple-element.76), channel_id=1, source_target_pairs={{0,8},{8,16},{16,24},{24,32},{32,40},{40,48},{48,56},{56,64},{64,7... | collective-permute-start | bytes 3080 | tf_op jit(solution)/shard_map/ppermute | solution.py:59
  294.9 6.0 %collective-permute-start.7 = (f32[2,128]{1,0:T(2,128)S(1)}, f32[2,128]{1,0:T(2,128)S(1)}, u32[]{:S(2)}, u32[]{:S(2)}) collective-permute-start(f32[2,128]{1,0:T(2,128)S(1)} %get-tuple-element.77), channel_id=1, source_target_pairs={{8,0},{16,8},{24,16},{32,24},{40,32},{48,40},{56,48},{64,56},{72,6... | collective-permute-start | bytes 3080 | tf_op jit(solution)/shard_map/ppermute | solution.py:61
  297.5 10.5 %all-to-all-start.5 = ((f32[8,2,1024]{2,1,0:T(2,128)}), f32[8,2,1024]{2,1,0:T(2,128)S(1)}, u32[]{:S(2)}, u32[]{:S(2)}) async-start(f32[8,2,1024]{2,1,0:T(2,128)} %broadcast_in_dim.44), calls=%async_computation.5 | async-start | bytes 131072 | tf_op jit(solution)/shard_map/all_to_all | solution.py:24
  315.5 11.0 %collective-permute-start.8 = (f32[2,128]{1,0:T(2,128)S(1)}, f32[2,128]{1,0:T(2,128)S(1)}, u32[]{:S(2)}, u32[]{:S(2)}) collective-permute-start(f32[2,128]{1,0:T(2,128)S(1)} %get-tuple-element.72), channel_id=1, source_target_pairs={{0,8},{8,16},{16,24},{24,32},{32,40},{40,48},{48,56},{56,64},{64,7... | collective-permute-start | bytes 3080 | tf_op jit(solution)/shard_map/ppermute | solution.py:59
  320.3 6.2 %collective-permute-start.9 = (f32[2,128]{1,0:T(2,128)S(1)}, f32[2,128]{1,0:T(2,128)S(1)}, u32[]{:S(2)}, u32[]{:S(2)}) collective-permute-start(f32[2,128]{1,0:T(2,128)S(1)} %get-tuple-element.73), channel_id=1, source_target_pairs={{8,0},{16,8},{24,16},{32,24},{40,32},{48,40},{56,48},{64,56},{72,6... | collective-permute-start | bytes 3080 | tf_op jit(solution)/shard_map/ppermute | solution.py:61
  322.8 10.7 %all-to-all-start.6 = ((f32[8,2,1024]{2,1,0:T(2,128)}), f32[8,2,1024]{2,1,0:T(2,128)S(1)}, u32[]{:S(2)}, u32[]{:S(2)}) async-start(f32[8,2,1024]{2,1,0:T(2,128)} %broadcast_in_dim.45), calls=%async_computation.6 | async-start | bytes 131072 | tf_op jit(solution)/shard_map/all_to_all | solution.py:24
  341.1 10.7 %collective-permute-start.10 = (f32[2,128]{1,0:T(2,128)S(1)}, f32[2,128]{1,0:T(2,128)S(1)}, u32[]{:S(2)}, u32[]{:S(2)}) collective-permute-start(f32[2,128]{1,0:T(2,128)S(1)} %get-tuple-element.66), channel_id=1, source_target_pairs={{0,8},{8,16},{16,24},{24,32},{32,40},{40,48},{48,56},{56,64},{64,7... | collective-permute-start | bytes 3080 | tf_op jit(solution)/shard_map/ppermute | solution.py:59
  345.9 6.0 %collective-permute-start.11 = (f32[2,128]{1,0:T(2,128)S(1)}, f32[2,128]{1,0:T(2,128)S(1)}, u32[]{:S(2)}, u32[]{:S(2)}) collective-permute-start(f32[2,128]{1,0:T(2,128)S(1)} %get-tuple-element.67), channel_id=1, source_target_pairs={{8,0},{16,8},{24,16},{32,24},{40,32},{48,40},{56,48},{64,56},{72,6... | collective-permute-start | bytes 3080 | tf_op jit(solution)/shard_map/ppermute | solution.py:61
  348.5 10.5 %all-to-all-start.7 = ((f32[8,2,1024]{2,1,0:T(2,128)}), f32[8,2,1024]{2,1,0:T(2,128)S(1)}, u32[]{:S(2)}, u32[]{:S(2)}) async-start(f32[8,2,1024]{2,1,0:T(2,128)} %broadcast_in_dim.46), calls=%async_computation.7 | async-start | bytes 131072 | tf_op jit(solution)/shard_map/all_to_all | solution.py:24
  440.6 10.0 %all-to-all-start.8 = ((f32[8,1,34]{2,1,0:T(1,128)}), f32[8,1,34]{2,1,0:T(1,128)S(1)}, u32[]{:S(2)}, u32[]{:S(2)}) async-start(f32[8,1,34]{2,1,0:T(1,128)} %broadcast_in_dim.47), calls=%async_computation.8 | async-start | bytes 8192 | tf_op jit(solution)/shard_map/all_to_all | solution.py:24
  494.4 9.7 %all-to-all-start.9 = ((f32[8,1,1]{2,1,0:T(1,128)}), f32[8,1,1]{2,1,0:T(1,128)S(1)}, u32[]{:S(2)}, u32[]{:S(2)}) async-start(f32[8,1,1]{2,1,0:T(1,128)} %broadcast_in_dim.96), calls=%async_computation.9 | async-start | bytes 8192 | tf_op jit(solution)/shard_map/all_to_all | solution.py:24
  (1 other events, 15.9 us)
where the time goes:
time: 550 us; the launch traced here: 541 us
  blocking collectives  260 us (47%)
  starting transfers between devices  80.6 us (15%)
  matrix products  69.6 us (13%)
  waiting for transfers between devices  58 us (11%)
  between operations  40.2 us (7%)
  local copies, waits for them, and re-layouts  18.5 us (3%)
  other arithmetic  14 us (3%)
    psum x20, blocking collectives, one_axis_at_a_time(): array = lax.psum(array, axis)  260 us
    all_to_all x10, waiting for transfers between devices, from_everyone(): return lax.all_to_all(copies, axis, split_axis=0, concat_axis=0, tiled=True)  58 us
    all_to_all x10, starting transfers between devices, from_everyone(): return lax.all_to_all(copies, axis, split_axis=0, concat_axis=0, tiled=True)  34.4 us
    ppermute x6, starting transfers between devices, with_halo(): lax.ppermute(tail, axis, [(i, (i + 1) % count) for i in range(ends)])  25.1 us
    ppermute x6, starting transfers between devices, with_halo(): lax.ppermute(head, axis, [((i + 1) % count, i) for i in range(ends)])  21.1 us
  transfers between devices with their start and end apart: 22, of which 10 were waited for; matrix products, arithmetic and copies ran while one was open for 3% of the time, Pallas kernels for 0%

commit v1 on v0

v1 whole, which is shorter than its diff:
```python
import functools

import jax
import jax.numpy as jnp
from jax import lax
from jax.experimental import pallas as pl
from jax.experimental.pallas import tpu as pltpu
from jax.sharding import PartitionSpec as P

MESH = pl.DeviceIdType.MESH
HIGH = lax.Precision.HIGHEST
F32 = jnp.float32
BF16 = jnp.bfloat16
EPSILON = 1e-06

ITERS = 3
TD = 8
TILE = 128
NB = 16
CORES = 2
Z_CHIPS = 8

PREV, ZROW, UROW, RIGHT, XROWS = 32, 34, 40, 46, 128
NT_DIMS = (((1,), (1,)), ((), ()))


def halves(a):
    hi = a.astype(BF16)
    return hi, (a - hi.astype(F32)).astype(BF16)


def rows4(re, im):
    rh = re.astype(BF16).astype(F32)
    ih = im.astype(BF16).astype(F32)
    return jnp.concatenate([rh, ih, re - rh, im - ih], axis=0).astype(BF16)


def nt(a, b):
    return lax.dot_general(a, b, NT_DIMS, preferred_element_type=F32)


def own_columns(product, lanes):
    lane = lax.broadcasted_iota(jnp.int32, (TILE, lanes), 1) % TD
    total = jnp.zeros((TILE, lanes), F32)
    for t in range(TD):
        total = total + jnp.where(lane == t, product[t * TILE : (t + 1) * TILE], 0.0)
    return total


def fold(columns):
    rows = columns.T
    re, im = rows[0:8], rows[8:16]
    for at in range(16, rows.shape[0], 16):
        re = re + rows[at : at + 8]
        im = im + rows[at + 8 : at + 16]
    return re, im


def gram(top, bottom):
    th, tl = halves(top)
    bh, bl = halves(bottom)
    return nt(jnp.concatenate([th, tl, th, tl], axis=1), jnp.concatenate([bh, bh, bl, bl], axis=1))


def solve(entry):
    def g_re(a, b):
        return entry(2 * a, UROW + 2 * b) + entry(2 * a + 1, UROW + 2 * b + 1)

    def g_im(a, b):
        return entry(2 * a, UROW + 2 * b + 1) - entry(2 * a + 1, UROW + 2 * b)

    real, imag = {}, {}
    for a in range(ITERS):
        for b in range(a + 1):
            real[a, b] = real[b, a] = g_re(a, b)
            if a != b:
                imag[a, b] = g_im(a, b)
                imag[b, a] = -imag[a, b]
            else:
                imag[a, a] = jnp.zeros_like(real[a, a])
    order = 2 * ITERS
    matrix = {}
    for i in range(order):
        for j in range(i + 1):
            a, b = i % ITERS, j % ITERS
            matrix[i, j] = real[a, b] if (i < ITERS) == (j < ITERS) else imag[a, b]
    vector = [g_re(a, ITERS) for a in range(ITERS)] + [g_im(a, ITERS) for a in range(ITERS)]
    lower, inverse = {}, {}
    for i in range(order):
        for j in range(i + 1):
            value = matrix[i, j]
            for k in range(j):
                value = value - lower[i, k] * lower[j, k]
            if i == j:
                inverse[i] = 1.0 / jnp.sqrt(value)
            else:
                lower[i, j] = value * inverse[j]
    forward = []
    for i in range(order):
        value = vector[i]
        for k in range(i):
            value = value - lower[i, k] * forward[k]
        forward.append(value * inverse[i])
    result = [None] * order
    for i in reversed(range(order)):
        value = forward[i]
        for k in range(i + 1, order):
            value = value - lower[k, i] * result[k]
        result[i] = value * inverse[i]
    return result[:ITERS], result[ITERS:]


def kernel(
    sizes,
    pattern,
    c_rows,
    c_side,
    c_count,
    shifts,
    weights,
    compact,
    fresh,
    mass,
    basis,
    k_hbm,
    p_hbm,
    c_hbm,
    made,
    listed,
    k_raw,
    p_raw,
    c_raw,
    k_two,
    p_two,
    c_two,
    stack,
    coef_table,
    weight_rows,
    right_coef,
    basis_gram,
    picked,
    tiles0,
    tiles1,
    tiles2,
    halo,
    sums,
    load_sem,
    tile_send,
    tile_recv,
    halo_send,
    halo_recv,
    sum_send,
    sum_recv,
):
    ny, nz, nc, ns = sizes
    steps = weights.shape[0]
    total_rows = float(ny * nz * nc * ns * TD * TILE)
    n_dom = ny * nz * nc
    dom, sub = lax.axis_index("dom"), lax.axis_index("sub")
    core, chip_z, chip_y = dom % nc, (dom // nc) % nz, dom // (nc * nz)

    def at(y, z, c):
        return (y * nz + z) * nc + c

    def along(stage, d):
        if stage == 0:
            return (dom, (sub + d) % ns)
        if stage == 1:
            return (at((chip_y + d) % ny, chip_z, core), sub)
        if stage == 2:
            return (at(chip_y, (chip_z + d) % nz, core), sub)
        return (at(chip_y, chip_z, (core + d) % nc), sub)

    extents = (ns, ny, nz, nc)
    places = (sub, chip_y, chip_z, core)
    lower_dom, upper_dom = ((dom + n_dom - 1) % n_dom, sub), ((dom + 1) % n_dom, sub)

    loads = [
        pltpu.make_async_copy(basis.at[0], stack.at[pl.ds(0, NB)], load_sem.at[0]),
        pltpu.make_async_copy(basis.at[1], stack.at[pl.ds(NB, NB)], load_sem.at[1]),
        pltpu.make_async_copy(p_hbm, p_raw, load_sem.at[2]),
        pltpu.make_async_copy(k_hbm, k_raw, load_sem.at[3]),
        pltpu.make_async_copy(c_hbm, c_raw, load_sem.at[4]),
    ]
    for load in loads:
        load.start()

    barrier = pltpu.get_barrier_semaphore()
    greeted = 0
    for stage in range(4):
        for d in range(1, extents[stage]):
            pl.semaphore_signal(barrier, inc=1, device_id=along(stage, d), device_id_type=MESH)
            greeted += 1
    for who in (lower_dom, upper_dom):
        pl.semaphore_signal(barrier, inc=1, device_id=who, device_id_type=MESH)
        greeted += 1

    lane = lax.broadcasted_iota(jnp.int32, (8, TILE), 1)
    row = lax.broadcasted_iota(jnp.int32, (8, TILE), 0)

    coef_table[...] = jnp.zeros_like(coef_table)
    terms = compact.shape[1]
    coef_table[0:terms, 0:NB] = compact[0]
    coef_table[0:terms, NB : 2 * NB] = -compact[1]
    coef_table[terms : 2 * terms, 0:NB] = compact[1]
    coef_table[terms : 2 * terms, NB : 2 * NB] = compact[0]
    weight_rows[...] = jnp.zeros_like(weight_rows)
    for k in range(steps):
        weight_rows[2 * k : 2 * k + 1, 0:terms] = weights[k, 0:1, :]
        weight_rows[2 * k : 2 * k + 1, terms : 2 * terms] = -weights[k, 1:2, :]
        weight_rows[2 * k + 1 : 2 * k + 2, 0:terms] = weights[k, 1:2, :]
        weight_rows[2 * k + 1 : 2 * k + 2, terms : 2 * terms] = weights[k, 0:1, :]
    mixed_rows = jnp.dot(
        weight_rows[:, 0 : 2 * terms], coef_table[...], precision=HIGH, preferred_element_type=F32
    )
    for k in range(steps):
        wr, wi = weights[k, 0:1, :], weights[k, 1:2, :]
        fr, fi = fresh[0:1, :], fresh[1:2, :]
        gr = jnp.sum(wr * fr - wi * fi, axis=1, keepdims=True)
        gi = jnp.sum(wr * fi + wi * fr, axis=1, keepdims=True)
        line = lane[0:1]
        first = mixed_rows[2 * k : 2 * k + 1]
        second = mixed_rows[2 * k + 1 : 2 * k + 2]
        first = jnp.where(line == PREV, gr, jnp.where(line == PREV + 1, -gi, first))
        second = jnp.where(line == PREV, gi, jnp.where(line == PREV + 1, gr, second))
        right_coef[k] = jnp.zeros((8, TILE), F32)
        right_coef[k, 0:1, :] = first
        right_coef[k, 1:2, :] = second

    slot_lane = lax.broadcasted_iota(jnp.int32, (1, 64), 1)
    slot_masks = []
    for j in range(TD):
        live = j < c_count[0]
        present = jnp.where(c_side[j] == 0, (dom > 0).astype(jnp.int32), (dom < n_dom - 1).astype(jnp.int32))
        on = jnp.where(live, present, 0)
        hit = (slot_lane // 32 == c_side[j]) & (slot_lane % TD == c_rows[j])
        slot_masks.append(jnp.where(hit, on, 0).astype(F32))

    stack[pl.ds(PREV, XROWS - PREV), :] = jnp.zeros((XROWS - PREV, TD * TILE), F32)
    loads[0].wait()
    loads[1].wait()

    wide = gram(stack[0 : 2 * NB, :], stack[0:XROWS, :])
    basis_gram[...] = jnp.zeros_like(basis_gram)
    basis_gram[:, 0:XROWS] = wide
    upper, under = basis_gram[0:NB, :], basis_gram[NB : 2 * NB, :]
    lane2 = lax.broadcasted_iota(jnp.int32, (NB, TILE), 1)
    mixed = upper + jnp.where(lane2 < NB, pltpu.roll(under, TILE - NB, 1), -pltpu.roll(under, NB, 1))
    mixed = jnp.where(lane2 < 2 * NB, mixed, 0.0)
    basis_part = pltpu.roll(mixed[0:8], 64, 1) + pltpu.roll(mixed[8:16], 96, 1)

    loads[2].wait()

    @pl.loop(0, TD)
    def _(t):
        for c in range(2):
            hi, lo = halves(p_raw[t, c])
            p_two[pl.ds(t * TILE, TILE), (2 * c) * TILE : (2 * c + 1) * TILE] = hi
            p_two[pl.ds(t * TILE, TILE), (2 * c + 1) * TILE : (2 * c + 2) * TILE] = lo

    gathered = (tiles0, tiles1, tiles2)

    def split_rest():
        loads[3].wait()

        @pl.loop(0, TD)
        def _(t):
            for q in range(3):
                hi, lo = halves(k_raw[t, q])
                k_two[pl.ds(t * TILE, TILE), (2 * q) * TILE : (2 * q + 1) * TILE] = hi
                k_two[pl.ds(t * TILE, TILE), (2 * q + 1) * TILE : (2 * q + 2) * TILE] = lo

        loads[4].wait()

        @pl.loop(0, TD)
        def _(t):
            hi, lo = halves(c_raw[t])
            c_two[pl.ds(t * TILE, TILE), 0:TILE] = hi
            c_two[pl.ds(t * TILE, TILE), TILE : 2 * TILE] = lo

    def to_stack(at_row, re, im):
        for t in range(TD):
            stack[at_row : at_row + 1, t * TILE : (t + 1) * TILE] = re[t : t + 1]
            stack[at_row + 1 : at_row + 2, t * TILE : (t + 1) * TILE] = im[t : t + 1]

    def one_step(step):
        right = jnp.dot(
            right_coef[step][:, 0:UROW], stack[0:UROW, :], precision=HIGH, preferred_element_type=F32
        )
        stack[RIGHT : RIGHT + 2, :] = right[0:2]
        t_re = jnp.concatenate([right[0:1, t * TILE : (t + 1) * TILE] for t in range(TD)], axis=0)
        t_im = jnp.concatenate([right[1:2, t * TILE : (t + 1) * TILE] for t in range(TD)], axis=0)
        shift_re, shift_im = shifts[step, 0], shifts[step, 1]
        for it in range(ITERS):
            tiles = gathered[it]
            plain, turned = rows4(t_re, t_im), rows4(-t_im, t_re)
            product = nt(p_two[...], jnp.concatenate([plain, plain, turned, turned], axis=1))
            z_re, z_im = fold(own_columns(product, 32))
            tiles[sub, 0] = z_re
            tiles[sub, 1] = z_im
            if it == 0:

                @pl.when(step == 0)
                def _():
                    pl.semaphore_wait(barrier, greeted)

            copies = []
            for side, who in ((1, lower_dom), (0, upper_dom)):
                copies.append(
                    pltpu.make_async_remote_copy(
                        src_ref=tiles.at[sub],
                        dst_ref=halo.at[step * ITERS + it, side],
                        send_sem=halo_send.at[step * ITERS + it, side],
                        recv_sem=halo_recv.at[step * ITERS + it, side],
                        device_id=who,
                        device_id_type=MESH,
                    )
                )
            for d in range(1, ns):
                copies.append(
                    pltpu.make_async_remote_copy(
                        src_ref=tiles.at[sub],
                        dst_ref=tiles.at[sub],
                        send_sem=tile_send.at[step * ITERS + it, d],
                        recv_sem=tile_recv.at[step * ITERS + it, d],
                        device_id=along(0, d),
                        device_id_type=MESH,
                    )
                )
            for copy in copies:
                copy.start()
            if it == 0:

                @pl.when(step == 0)
                def _():
                    split_rest()

            to_stack(ZROW + 2 * it, z_re, z_im)
            own = rows4(z_re, z_im)
            columns = own_columns(nt(k_two[:, 0 : 2 * TILE], jnp.concatenate([own, own], axis=1)), 32)
            u_re, u_im = fold(columns)
            moved_re, moved_im = mass[...] * z_re, mass[...] * z_im
            u_re = u_re - (shift_re * moved_re - shift_im * moved_im)
            u_im = u_im - (shift_re * moved_im + shift_im * moved_re)

            copies[0].wait_recv()
            copies[1].wait_recv()
            sides = []
            for side, tile in ((0, TD - 1), (1, 0)):
                re = jnp.broadcast_to(halo[step * ITERS + it, side, 0, tile : tile + 1, :], (8, TILE))
                im = jnp.broadcast_to(halo[step * ITERS + it, side, 1, tile : tile + 1, :], (8, TILE))
                sides.append(rows4(re, im))
            rims = jnp.concatenate(sides, axis=0)
            product = nt(c_two[...], jnp.concatenate([rims, rims], axis=1))
            columns = jnp.zeros((TILE, 64), F32)
            for j in range(TD):
                columns = columns + slot_masks[j] * product[j * TILE : (j + 1) * TILE]
            c_re, c_im = fold(columns)
            u_re, u_im = u_re + c_re, u_im + c_im

            for copy in copies[2:]:
                copy.wait_recv()
            for q in range(2):
                for t in range(TD):
                    source = pattern[t, q]
                    for c in range(2):
                        picked[q, c, t : t + 1, :] = tiles[source // TD, c, pl.ds(source % TD, 1), :]
            first = rows4(picked[0, 0], picked[0, 1])
            second = rows4(picked[1, 0], picked[1, 1])
            product = nt(k_two[:, 2 * TILE :], jnp.concatenate([first, first, second, second], axis=1))
            k_re, k_im = fold(own_columns(product, 32))
            u_re, u_im = u_re + k_re, u_im + k_im
            to_stack(UROW + 2 * it, u_re, u_im)
            t_re, t_im = u_re - t_re, u_im - t_im
            for copy in copies:
                copy.wait_send()

        both = gram(stack[PREV:48, :], stack[0:XROWS, :])
        narrow = lax.broadcasted_iota(jnp.int32, (8, XROWS), 1)
        sums[step, 0, sub] = basis_part
        sums[step, 0, sub] = jnp.where(narrow < UROW, both[0:8], jnp.where(narrow < 48, both[8:16], basis_part))
        for stage in range(4):
            place = places[stage]
            copies = []
            for d in range(1, extents[stage]):
                copies.append(
                    pltpu.make_async_remote_copy(
                        src_ref=sums.at[step, stage, place],
                        dst_ref=sums.at[step, stage, place],
                        send_sem=sum_send.at[step, stage, d],
                        recv_sem=sum_recv.at[step, stage, d],
                        device_id=along(stage, d),
                        device_id_type=MESH,
                    )
                )
            for copy in copies:
                copy.start()
            for copy in copies:
                copy.wait_recv()
            reduced = sums[step, stage, 0]
            for other in range(1, extents[stage]):
                reduced = reduced + sums[step, stage, other]
            if stage < 3:
                sums[step, stage + 1, places[stage + 1]] = reduced
            for copy in copies:
                copy.wait_send()

        def entry(i, j):
            return jnp.broadcast_to(reduced[i : i + 1, j : j + 1], (8, TILE))

        def line_of(i):
            return jnp.broadcast_to(reduced[i : i + 1, :], (8, TILE))

        y_re, y_im = solve(entry)
        with_re = jnp.zeros((8, TILE), F32)
        with_im = jnp.zeros((8, TILE), F32)
        sol_re = jnp.zeros((8, TILE), F32)
        sol_im = jnp.zeros((8, TILE), F32)
        for j in range(ITERS):
            a, b = line_of(2 + 2 * j), line_of(3 + 2 * j)
            with_re = with_re + (y_re[j] * a - y_im[j] * b)
            with_im = with_im + (y_re[j] * b + y_im[j] * a)
            here, after = lane == ZROW + 2 * j, lane == ZROW + 2 * j + 1
            sol_re = jnp.where(here, y_re[j], jnp.where(after, -y_im[j], sol_re))
            sol_im = jnp.where(here, y_im[j], jnp.where(after, y_re[j], sol_im))

        def back(a, n):
            return pltpu.roll(a, TILE - n, 1)

        on_basis, on_prev = lane < NB, lane == PREV
        h_re = jnp.where(
            on_basis, with_re + back(with_im, NB), jnp.where(on_prev, with_re + back(with_im, 1), 0.0)
        )
        h_im = jnp.where(
            on_basis, with_im - back(with_re, NB), jnp.where(on_prev, with_im - back(with_re, 1), 0.0)
        )
        h_re, h_im = h_re / total_rows, h_im / total_rows
        on_imag, on_prev_imag = (lane >= NB) & (lane < 2 * NB), lane == PREV + 1
        e_re = h_re - jnp.where(
            on_imag, pltpu.roll(h_im, NB, 1), jnp.where(on_prev_imag, pltpu.roll(h_im, 1, 1), 0.0)
        )
        e_im = h_im + jnp.where(
            on_imag, pltpu.roll(h_re, NB, 1), jnp.where(on_prev_imag, pltpu.roll(h_re, 1, 1), 0.0)
        )

        @pl.when(step == 0)
        def _():
            basis_gram[0:8, :] = jnp.where(lane < 2 * NB, pltpu.roll(reduced, 64, 1), 0.0)
            basis_gram[8:16, :] = jnp.where(lane < 2 * NB, pltpu.roll(reduced, 32, 1), 0.0)

        pair = jnp.where(row == 0, e_re, jnp.where(row == 1, e_im, 0.0))
        turned = jnp.dot(pair[:, 0:NB], basis_gram[0:NB, :], precision=HIGH, preferred_element_type=F32)
        p_re = jnp.broadcast_to(h_re[0:1, PREV : PREV + 1], (8, TILE))
        p_im = jnp.broadcast_to(h_im[0:1, PREV : PREV + 1], (8, TILE))
        prev_re, prev_im = line_of(0), line_of(1)
        v_re, v_im = p_re * prev_re - p_im * prev_im, p_im * prev_re + p_re * prev_im
        share = jnp.where(lane < PREV, 2.0, jnp.where(lane < PREV + 2, 1.0, 0.0))
        first_row = (
            sol_re * with_re
            + sol_im * with_im
            - 2.0 * total_rows * (h_re * h_re + h_im * h_im)
            + share * (v_re * e_re + v_im * e_im)
        )
        first_row = jnp.where(lane < UROW, first_row, 0.0)
        each = turned * pair + jnp.where(row == 0, first_row, 0.0)
        squares = jnp.sum(jnp.sum(each, axis=0, keepdims=True), axis=1, keepdims=True)
        squares = jnp.broadcast_to(squares, (8, TILE))
        norm = jnp.sqrt(jnp.maximum(squares, 0.0) / total_rows + EPSILON)

        coef = jnp.where(row == 0, sol_re - e_re, jnp.where(row == 1, sol_im - e_im, 0.0)) / norm
        latest = jnp.dot(coef[:, 0:UROW], stack[0:UROW, :], precision=HIGH, preferred_element_type=F32)
        made[step] = latest[0:2]
        stack[PREV : PREV + 2, :] = latest[0:2]
        top = jnp.where(on_basis, h_re, jnp.where(lane == NB, back(h_re, NB), norm))
        low = jnp.where(on_basis, h_im, jnp.where(lane == NB, back(h_im, NB), 0.0))
        listed[step, 0:1, :] = top[0:1, 0 : NB + 2]
        listed[step, 1:2, :] = low[0:1, 0 : NB + 2]

    @pl.loop(0, steps)
    def _(step):
        one_step(step)


def solution(mesh, y_chips=None):
    ns, n_dom = mesh.shape["sub"], mesh.shape["dom"]
    nz = Z_CHIPS if y_chips is None else n_dom // CORES // y_chips
    sizes = (n_dom // (CORES * nz), nz, CORES, ns)
    most = max(sizes)

    def local(basis, compact, weights, fresh, shifts, k_tiles, pattern, mass, precond, c_tiles, c_rows, c_side, c_count):
        smem = pl.BlockSpec(memory_space=pltpu.SMEM)
        vmem = pl.BlockSpec(memory_space=pltpu.VMEM)
        anywhere = pl.BlockSpec(memory_space=pl.ANY)
        steps = weights.shape[0]
        rows = TD * TILE
        return pl.pallas_call(
            functools.partial(kernel, sizes),
            out_shape=(
                jax.ShapeDtypeStruct((steps, 2, rows), F32),
                jax.ShapeDtypeStruct((steps, 2, NB + 2), F32),
            ),
            in_specs=[smem] * 5 + [vmem] * 4 + [anywhere] * 4,
            out_specs=(vmem, vmem),
            scratch_shapes=[
                pltpu.VMEM((TD, 3, TILE, TILE), F32),
                pltpu.VMEM((TD, 2, TILE, TILE), F32),
                pltpu.VMEM((TD, TILE, TILE), F32),
                pltpu.VMEM((rows, 6 * TILE), BF16),
                pltpu.VMEM((rows, 4 * TILE), BF16),
                pltpu.VMEM((rows, 2 * TILE), BF16),
                pltpu.VMEM((XROWS, rows), F32),
                pltpu.VMEM((2 * weights.shape[2], TILE), F32),
                pltpu.VMEM((8, TILE), F32),
                pltpu.VMEM((steps, 8, TILE), F32),
                pltpu.VMEM((2 * NB, TILE), F32),
                pltpu.VMEM((2, 2, TD, TILE), F32),
                pltpu.VMEM((ns, 2, TD, TILE), F32),
                pltpu.VMEM((ns, 2, TD, TILE), F32),
                pltpu.VMEM((ns, 2, TD, TILE), F32),
                pltpu.VMEM((steps * ITERS, 2, 2, TD, TILE), F32),
                pltpu.VMEM((steps, 4, most, 8, TILE), F32),
                pltpu.SemaphoreType.DMA((5,)),
                pltpu.SemaphoreType.DMA((steps * ITERS, ns)),
                pltpu.SemaphoreType.DMA((steps * ITERS, ns)),
                pltpu.SemaphoreType.DMA((steps * ITERS, 2)),
                pltpu.SemaphoreType.DMA((steps * ITERS, 2)),
                pltpu.SemaphoreType.DMA((steps, 4, most)),
                pltpu.SemaphoreType.DMA((steps, 4, most)),
            ],
            compiler_params=pltpu.CompilerParams(collective_id=0, has_side_effects=True),
        )(
            pattern,
            c_rows,
            c_side,
            c_count,
            shifts,
            weights,
            compact,
            fresh,
            mass.reshape(TD, TILE),
            basis,
            k_tiles,
            precond,
            c_tiles,
        )

    both = ("dom", "sub")
    placed = (
        P(None, None, both),
        P(),
        P(),
        P(),
        P(),
        P(both, None, None, None),
        P(both, None),
        P(both),
        P(both, None, None, None),
        P(both, None, None),
        P(both),
        P(both),
        P(both),
    )
    return jax.shard_map(
        local, mesh=mesh, in_specs=placed, out_specs=(P(None, None, both), P()), check_vma=False
    )
```

time: 550 us -> 106 us (0.19); the launches traced: 541 us -> 105 us
  blocking collectives: 260 us -> 0 us
  Pallas kernels: 0 us -> 98.6 us
  starting transfers between devices: 80.6 us -> 0 us
  matrix products: 69.6 us -> 0 us
  waiting for transfers between devices: 58 us -> 0 us
  between operations: 40.2 us -> 1.29 us
  other arithmetic: 14 us -> 0 us
  local copies, waits for them, and re-layouts: 18.5 us -> 5.31 us
    psum x20 -> x0, blocking collectives: 260 us -> none  [one_axis_at_a_time(): array = lax.psum(array, axis)]
    pallas_call x0 -> x1, Pallas kernels: none -> 98.6 us  [local(): pl.pallas_call(functools.partial(kernel, sizes), out_shape=(jax.ShapeDtyp...]
    dot_general x98 -> x0, matrix products: 69.6 us -> none  [the longest x6 10.7 us: local(): jnp.einsum('tsij,ctsj->cti', k_tiles, blocks[:, columns], precision=HIGH)]
    all_to_all x10 -> x0, waiting for transfers between devices: 58 us -> none  [from_everyone(): return lax.all_to_all(copies, axis, split_axis=0, concat_axis=0, tiled=True)]
    ppermute x12 -> x0, starting transfers between devices: 46.2 us -> none  [the longest x6 25.1 us: with_halo(): lax.ppermute(tail, axis, [(i, (i + 1) % count) for i in range(ends)])]
    all_to_all x10 -> x0, starting transfers between devices: 34.4 us -> none  [from_everyone(): return lax.all_to_all(copies, axis, split_axis=0, concat_axis=0, tiled=True)]
    sub x24 -> x0, other arithmetic: 7.73 us -> none  [the longest x6 7.55 us: apply_shift(): real = stiff[0] - (shift_pair[0] * moved_real - shift_pair[1] * moved_imag)]
    broadcast_in_dim x10 -> x0, local copies, waits for them, and re-layouts: 7.47 us -> none  [from_everyone(): copies = jnp.broadcast_to(array, (lax.axis_size(axis), *array.shape))]
  transfers between devices with their start and end apart: 22 -> 0, of which waited for: 10 -> 0; matrix products, arithmetic and copies ran while one was open for 3% -> 0% of each run, Pallas kernels for 0% -> 0%
where the time goes in v1:
time: 106 us; the launch traced here: 105 us
  Pallas kernels  98.6 us (93%)
  local copies, waits for them, and re-layouts  5.31 us (5%)
  between operations  1.29 us (1%)
    pallas_call x1, Pallas kernels, local(): pl.pallas_call(functools.partial(kernel, sizes), out_shape=(jax.ShapeDtyp...  98.6 us
    unnamed x4, local copies, waits for them, and re-layouts  5.31 us

profile of v1, /device:TPU:1, one launch (start us, length us, event | category | flops | bytes accessed | tf_op | source)
XLA Modules:
  0.0 105.2 jit_solution(10568523252385383002)
XLA Ops:
  1.3 1.3 %copy.15.pattern = s32[8,2]{1,0:T(8,128)} copy(s32[8,2]{0,1:T(2,128)} %param.19) | data formatting | bytes 128 | tf_op args[6]
  2.6 1.4 %copy.16.compact = f32[2,32,16]{2,1,0:T(8,128)} copy(f32[2,32,16]{1,2,0:T(8,128)} %param.14) | data formatting | bytes 8192 | tf_op args[1]
  4.0 98.6 %shard_map.140 = (f32[2,2,1024]{2,1,0:T(2,128)}, f32[2,2,18]{2,1,0:T(2,128)}) custom-call(s32[8,2]{1,0:T(8,128)} %copy.15.pattern, s32[8]{0:T(128)} %c_rows.1, s32[8]{0:T(128)} %c_side.1, s32[1]{0:T(128)S(6)} %copy.19.c_count, f32[2,2]{1,0:T(2,128)} %shifts.1, f32[2,2,32]{2,1,0:T(2,128)} %weights.1, f32[2,32,16]{2,1,0:T(8,128)} %copy.16.compact, ...), custom_call_target="tpu_custom_call" | custom-call | tf_op jit(solution)/shard_map/pallas_call | solution.py:496
  102.6 1.3 %copy.20 = f32[2,2,1024]{2,1,0:T(2,128)} copy(f32[2,2,1024]{2,1,0:T(2,128)} %get-tuple-element.4) | data formatting | bytes 32768
  103.9 1.2 %copy.21 = f32[2,2,18]{2,1,0:T(2,128)} copy(f32[2,2,18]{2,1,0:T(2,128)} %get-tuple-element.5) | data formatting | bytes 576

commit v2 on v1

--- a/solution.py
+++ b/solution.py
@@ -144,6 +144,8 @@
     tiles2,
     halo,
     sums,
+    basis_sums,
+    slot_masks,
     load_sem,
     tile_send,
     tile_recv,
@@ -151,6 +153,8 @@
     halo_recv,
     sum_send,
     sum_recv,
+    basis_send,
+    basis_recv,
 ):
     ny, nz, nc, ns = sizes
     steps = weights.shape[0]
@@ -167,12 +171,35 @@
             return (dom, (sub + d) % ns)
         if stage == 1:
             return (at((chip_y + d) % ny, chip_z, core), sub)
-        if stage == 2:
-            return (at(chip_y, (chip_z + d) % nz, core), sub)
-        return (at(chip_y, chip_z, (core + d) % nc), sub)
-
-    extents = (ns, ny, nz, nc)
-    places = (sub, chip_y, chip_z, core)
+        return (at(chip_y, (chip_z + d // nc) % nz, (core + d) % nc), sub)
+
+    extents = (ns, ny, nz * nc)
+    places = (sub, chip_y, chip_z * nc + core)
+    stages = len(extents)
+
+    def send_sum(store, prefix, send_sem, recv_sem, stage):
+        mine = store.at[(*prefix, stage, places[stage])]
+        for d in range(1, extents[stage]):
+            pltpu.make_async_remote_copy(
+                src_ref=mine,
+                dst_ref=mine,
+                send_sem=send_sem.at[(*prefix, stage)],
+                recv_sem=recv_sem.at[(*prefix, stage)],
+                device_id=along(stage, d),
+                device_id_type=MESH,
+            ).start()
+
+    def wait_for(ref, sem):
+        pltpu.make_async_copy(ref, ref, sem).wait()
+
+    def finish_sum(store, prefix, send_sem, recv_sem, stage):
+        others = store.at[(*prefix, stage, pl.ds(0, extents[stage] - 1))]
+        wait_for(others, recv_sem.at[(*prefix, stage)])
+        total = store[(*prefix, stage, 0)]
+        for other in range(1, extents[stage]):
+            total = total + store[(*prefix, stage, other)]
+        wait_for(others, send_sem.at[(*prefix, stage)])
+        return total
     lower_dom, upper_dom = ((dom + n_dom - 1) % n_dom, sub), ((dom + 1) % n_dom, sub)
 
     loads = [
@@ -187,7 +214,7 @@
 
     barrier = pltpu.get_barrier_semaphore()
     greeted = 0
-    for stage in range(4):
+    for stage in range(stages):
         for d in range(1, extents[stage]):
             pl.semaphore_signal(barrier, inc=1, device_id=along(stage, d), device_id_type=MESH)
             greeted += 1
@@ -197,21 +224,22 @@
 
     lane = lax.broadcasted_iota(jnp.int32, (8, TILE), 1)
     row = lax.broadcasted_iota(jnp.int32, (8, TILE), 0)
-
+    lane2 = lax.broadcasted_iota(jnp.int32, (NB, TILE), 1)
+
+    terms = weights.shape[2]
     coef_table[...] = jnp.zeros_like(coef_table)
-    terms = compact.shape[1]
-    coef_table[0:terms, 0:NB] = compact[0]
-    coef_table[0:terms, NB : 2 * NB] = -compact[1]
-    coef_table[terms : 2 * terms, 0:NB] = compact[1]
-    coef_table[terms : 2 * terms, NB : 2 * NB] = compact[0]
+    coef_table[0:NB, 0:terms] = compact[0]
+    coef_table[0:NB, terms : 2 * terms] = compact[1]
+    coef_table[NB : 2 * NB, 0:terms] = -compact[1]
+    coef_table[NB : 2 * NB, terms : 2 * terms] = compact[0]
     weight_rows[...] = jnp.zeros_like(weight_rows)
     for k in range(steps):
         weight_rows[2 * k : 2 * k + 1, 0:terms] = weights[k, 0:1, :]
         weight_rows[2 * k : 2 * k + 1, terms : 2 * terms] = -weights[k, 1:2, :]
         weight_rows[2 * k + 1 : 2 * k + 2, 0:terms] = weights[k, 1:2, :]
         weight_rows[2 * k + 1 : 2 * k + 2, terms : 2 * terms] = weights[k, 0:1, :]
-    mixed_rows = jnp.dot(
-        weight_rows[:, 0 : 2 * terms], coef_table[...], precision=HIGH, preferred_element_type=F32
+    mixed_rows = lax.dot_general(
+        weight_rows[...], coef_table[...], NT_DIMS, precision=HIGH, preferred_element_type=F32
     )
     for k in range(steps):
         wr, wi = weights[k, 0:1, :], weights[k, 1:2, :]
@@ -227,27 +255,9 @@
         right_coef[k, 0:1, :] = first
         right_coef[k, 1:2, :] = second
 
-    slot_lane = lax.broadcasted_iota(jnp.int32, (1, 64), 1)
-    slot_masks = []
-    for j in range(TD):
-        live = j < c_count[0]
-        present = jnp.where(c_side[j] == 0, (dom > 0).astype(jnp.int32), (dom < n_dom - 1).astype(jnp.int32))
-        on = jnp.where(live, present, 0)
-        hit = (slot_lane // 32 == c_side[j]) & (slot_lane % TD == c_rows[j])
-        slot_masks.append(jnp.where(hit, on, 0).astype(F32))
-
-    stack[pl.ds(PREV, XROWS - PREV), :] = jnp.zeros((XROWS - PREV, TD * TILE), F32)
+    stack[pl.ds(PREV, 16), :] = jnp.zeros((16, TD * TILE), F32)
     loads[0].wait()
     loads[1].wait()
-
-    wide = gram(stack[0 : 2 * NB, :], stack[0:XROWS, :])
-    basis_gram[...] = jnp.zeros_like(basis_gram)
-    basis_gram[:, 0:XROWS] = wide
-    upper, under = basis_gram[0:NB, :], basis_gram[NB : 2 * NB, :]
-    lane2 = lax.broadcasted_iota(jnp.int32, (NB, TILE), 1)
-    mixed = upper + jnp.where(lane2 < NB, pltpu.roll(under, TILE - NB, 1), -pltpu.roll(under, NB, 1))
-    mixed = jnp.where(lane2 < 2 * NB, mixed, 0.0)
-    basis_part = pltpu.roll(mixed[0:8], 64, 1) + pltpu.roll(mixed[8:16], 96, 1)
 
     loads[2].wait()
 
@@ -259,6 +269,29 @@
             p_two[pl.ds(t * TILE, TILE), (2 * c + 1) * TILE : (2 * c + 2) * TILE] = lo
 
     gathered = (tiles0, tiles1, tiles2)
+
+    def late_start():
+        slot_lane = lax.broadcasted_iota(jnp.int32, (1, 64), 1)
+        for j in range(TD):
+            live = j < c_count[0]
+            present = jnp.where(c_side[j] == 0, (dom > 0).astype(jnp.int32), (dom < n_dom - 1).astype(jnp.int32))
+            on = jnp.where(live, present, 0)
+            hit = (slot_lane // 32 == c_side[j]) & (slot_lane % TD == c_rows[j])
+            slot_masks[j : j + 1, :] = jnp.where(hit, on, 0).astype(F32)
+
+        stack[pl.ds(PREV + 16, XROWS - PREV - 16), :] = jnp.zeros((XROWS - PREV - 16, TD * TILE), F32)
+        wide = gram(stack[0 : 2 * NB, :], stack[0:XROWS, :])
+        basis_gram[...] = jnp.zeros_like(basis_gram)
+        basis_gram[:, 0:XROWS] = wide
+        upper, under = basis_gram[0:NB, :], basis_gram[NB : 2 * NB, :]
+        mixed = upper + jnp.where(lane2 < NB, pltpu.roll(under, TILE - NB, 1), -pltpu.roll(under, NB, 1))
+        mixed = jnp.where(lane2 < 2 * NB, mixed, 0.0)
+        basis_part = (
+            mixed[0:4] + pltpu.roll(mixed[4:8], 32, 1) + pltpu.roll(mixed[8:12], 64, 1) + pltpu.roll(mixed[12:16], 96, 1)
+        )
+        basis_sums[0, places[0]] = basis_part
+
+        send_sum(basis_sums, (), basis_send, basis_recv, 0)
 
     def split_rest():
         loads[3].wait()
@@ -304,36 +337,39 @@
                 def _():
                     pl.semaphore_wait(barrier, greeted)
 
-            copies = []
+            turn = step * ITERS + it
             for side, who in ((1, lower_dom), (0, upper_dom)):
-                copies.append(
-                    pltpu.make_async_remote_copy(
-                        src_ref=tiles.at[sub],
-                        dst_ref=halo.at[step * ITERS + it, side],
-                        send_sem=halo_send.at[step * ITERS + it, side],
-                        recv_sem=halo_recv.at[step * ITERS + it, side],
-                        device_id=who,
-                        device_id_type=MESH,
-                    )
-                )
+                pltpu.make_async_remote_copy(
+                    src_ref=tiles.at[sub],
+                    dst_ref=halo.at[turn, side],
+                    send_sem=halo_send.at[turn],
+                    recv_sem=halo_recv.at[turn],
+                    device_id=who,
+                    device_id_type=MESH,
+                ).start()
             for d in range(1, ns):
-                copies.append(
-                    pltpu.make_async_remote_copy(
-                        src_ref=tiles.at[sub],
-                        dst_ref=tiles.at[sub],
-                        send_sem=tile_send.at[step * ITERS + it, d],
-                        recv_sem=tile_recv.at[step * ITERS + it, d],
-                        device_id=along(0, d),
-                        device_id_type=MESH,
-                    )
-                )
-            for copy in copies:
-                copy.start()
+                pltpu.make_async_remote_copy(
+                    src_ref=tiles.at[sub],
+                    dst_ref=tiles.at[sub],
+                    send_sem=tile_send.at[turn],
+                    recv_sem=tile_recv.at[turn],
+                    device_id=along(0, d),
+                    device_id_type=MESH,
+                ).start()
             if it == 0:
 
                 @pl.when(step == 0)
                 def _():
                     split_rest()
+                    late_start()
+
+            else:
+
+                @pl.when(step == 0)
+                def _():
+                    so_far = finish_sum(basis_sums, (), basis_send, basis_recv, it - 1)
+                    basis_sums[it, places[it]] = so_far
+                    send_sum(basis_sums, (), basis_send, basis_recv, it)
 
             to_stack(ZROW + 2 * it, z_re, z_im)
             own = rows4(z_re, z_im)
@@ -343,26 +379,24 @@
             u_re = u_re - (shift_re * moved_re - shift_im * moved_im)
             u_im = u_im - (shift_re * moved_im + shift_im * moved_re)
 
-            copies[0].wait_recv()
-            copies[1].wait_recv()
+            wait_for(halo.at[turn], halo_recv.at[turn])
             sides = []
             for side, tile in ((0, TD - 1), (1, 0)):
-                re = jnp.broadcast_to(halo[step * ITERS + it, side, 0, tile : tile + 1, :], (8, TILE))
-                im = jnp.broadcast_to(halo[step * ITERS + it, side, 1, tile : tile + 1, :], (8, TILE))
+                re = jnp.broadcast_to(halo[turn, side, 0, tile : tile + 1, :], (8, TILE))
+                im = jnp.broadcast_to(halo[turn, side, 1, tile : tile + 1, :], (8, TILE))
                 sides.append(rows4(re, im))
             rims = jnp.concatenate(sides, axis=0)
             product = nt(c_two[...], jnp.concatenate([rims, rims], axis=1))
             columns = jnp.zeros((TILE, 64), F32)
             for j in range(TD):
-                columns = columns + slot_masks[j] * product[j * TILE : (j + 1) * TILE]
+                columns = columns + slot_masks[j : j + 1, :] * product[j * TILE : (j + 1) * TILE]
             c_re, c_im = fold(columns)
             u_re, u_im = u_re + c_re, u_im + c_im
 
-            for copy in copies[2:]:
-                copy.wait_recv()
+            wait_for(tiles.at[pl.ds(0, ns - 1)], tile_recv.at[turn])
             for q in range(2):
                 for t in range(TD):
-                    source = pattern[t, q]
+                    source = pattern[q, t]
                     for c in range(2):
                         picked[q, c, t : t + 1, :] = tiles[source // TD, c, pl.ds(source % TD, 1), :]
             first = rows4(picked[0, 0], picked[0, 1])
@@ -372,38 +406,17 @@
             u_re, u_im = u_re + k_re, u_im + k_im
             to_stack(UROW + 2 * it, u_re, u_im)
             t_re, t_im = u_re - t_re, u_im - t_im
-            for copy in copies:
-                copy.wait_send()
+            wait_for(halo.at[turn], halo_send.at[turn])
+            wait_for(tiles.at[pl.ds(0, ns - 1)], tile_send.at[turn])
 
         both = gram(stack[PREV:48, :], stack[0:XROWS, :])
-        narrow = lax.broadcasted_iota(jnp.int32, (8, XROWS), 1)
-        sums[step, 0, sub] = basis_part
-        sums[step, 0, sub] = jnp.where(narrow < UROW, both[0:8], jnp.where(narrow < 48, both[8:16], basis_part))
-        for stage in range(4):
-            place = places[stage]
-            copies = []
-            for d in range(1, extents[stage]):
-                copies.append(
-                    pltpu.make_async_remote_copy(
-                        src_ref=sums.at[step, stage, place],
-                        dst_ref=sums.at[step, stage, place],
-                        send_sem=sum_send.at[step, stage, d],
-                        recv_sem=sum_recv.at[step, stage, d],
-                        device_id=along(stage, d),
-                        device_id_type=MESH,
-                    )
-                )
-            for copy in copies:
-                copy.start()
-            for copy in copies:
-                copy.wait_recv()
-            reduced = sums[step, stage, 0]
-            for other in range(1, extents[stage]):
-                reduced = reduced + sums[step, stage, other]
-            if stage < 3:
-                sums[step, stage + 1, places[stage + 1]] = reduced
-            for copy in copies:
-                copy.wait_send()
+        packed = jnp.where(lane < UROW, both[0:8], jnp.where(lane < RIGHT + 2, both[8:16], 0.0))
+        part = packed[0:4] + pltpu.roll(packed[4:8], 64, 1)
+        for stage in range(stages):
+            sums[step, stage, places[stage]] = part
+            send_sum(sums, (step,), sum_send, sum_recv, stage)
+            part = finish_sum(sums, (step,), sum_send, sum_recv, stage)
+        reduced = jnp.concatenate([part, pltpu.roll(part, 64, 1)], axis=0)
 
         def entry(i, j):
             return jnp.broadcast_to(reduced[i : i + 1, j : j + 1], (8, TILE))
@@ -445,8 +458,9 @@
 
         @pl.when(step == 0)
         def _():
-            basis_gram[0:8, :] = jnp.where(lane < 2 * NB, pltpu.roll(reduced, 64, 1), 0.0)
-            basis_gram[8:16, :] = jnp.where(lane < 2 * NB, pltpu.roll(reduced, 32, 1), 0.0)
+            whole = finish_sum(basis_sums, (), basis_send, basis_recv, stages - 1)
+            blocks = [whole] + [pltpu.roll(whole, TILE - shift, 1) for shift in (32, 64, 96)]
+            basis_gram[0:NB, :] = jnp.where(lane2 < 2 * NB, jnp.concatenate(blocks, axis=0), 0.0)
 
         pair = jnp.where(row == 0, e_re, jnp.where(row == 1, e_im, 0.0))
         turned = jnp.dot(pair[:, 0:NB], basis_gram[0:NB, :], precision=HIGH, preferred_element_type=F32)
@@ -485,7 +499,7 @@
     ns, n_dom = mesh.shape["sub"], mesh.shape["dom"]
     nz = Z_CHIPS if y_chips is None else n_dom // CORES // y_chips
     sizes = (n_dom // (CORES * nz), nz, CORES, ns)
-    most = max(sizes)
+    most = max(ns, sizes[0], nz * CORES)
 
     def local(basis, compact, weights, fresh, shifts, k_tiles, pattern, mass, precond, c_tiles, c_rows, c_side, c_count):
         smem = pl.BlockSpec(memory_space=pltpu.SMEM)
@@ -509,7 +523,7 @@
                 pltpu.VMEM((rows, 4 * TILE), BF16),
                 pltpu.VMEM((rows, 2 * TILE), BF16),
                 pltpu.VMEM((XROWS, rows), F32),
-                pltpu.VMEM((2 * weights.shape[2], TILE), F32),
+                pltpu.VMEM((TILE, TILE), F32),
                 pltpu.VMEM((8, TILE), F32),
                 pltpu.VMEM((steps, 8, TILE), F32),
                 pltpu.VMEM((2 * NB, TILE), F32),
@@ -518,24 +532,28 @@
                 pltpu.VMEM((ns, 2, TD, TILE), F32),
                 pltpu.VMEM((ns, 2, TD, TILE), F32),
                 pltpu.VMEM((steps * ITERS, 2, 2, TD, TILE), F32),
-                pltpu.VMEM((steps, 4, most, 8, TILE), F32),
+                pltpu.VMEM((steps, 3, most, 4, TILE), F32),
+                pltpu.VMEM((3, most, 4, TILE), F32),
+                pltpu.VMEM((TD, 64), F32),
                 pltpu.SemaphoreType.DMA((5,)),
-                pltpu.SemaphoreType.DMA((steps * ITERS, ns)),
-                pltpu.SemaphoreType.DMA((steps * ITERS, ns)),
-                pltpu.SemaphoreType.DMA((steps * ITERS, 2)),
-                pltpu.SemaphoreType.DMA((steps * ITERS, 2)),
-                pltpu.SemaphoreType.DMA((steps, 4, most)),
-                pltpu.SemaphoreType.DMA((steps, 4, most)),
+                pltpu.SemaphoreType.DMA((steps * ITERS,)),
+                pltpu.SemaphoreType.DMA((steps * ITERS,)),
+                pltpu.SemaphoreType.DMA((steps * ITERS,)),
+                pltpu.SemaphoreType.DMA((steps * ITERS,)),
+                pltpu.SemaphoreType.DMA((steps, 3)),
+                pltpu.SemaphoreType.DMA((steps, 3)),
+                pltpu.SemaphoreType.DMA((3,)),
+                pltpu.SemaphoreType.DMA((3,)),
             ],
             compiler_params=pltpu.CompilerParams(collective_id=0, has_side_effects=True),
         )(
-            pattern,
+            pattern.T,
             c_rows,
             c_side,
             c_count,
             shifts,
             weights,
-            compact,
+            jnp.swapaxes(compact, 1, 2),
             fresh,
             mass.reshape(TD, TILE),
             basis,

time: 106 us -> 97.9 us (0.924)
  Pallas kernels: 98.6 us -> 93.8 us
  local copies, waits for them, and re-layouts: 5.31 us -> 2.55 us
    pallas_call x1, Pallas kernels: 98.6 us -> 93.8 us  [local(): pl.pallas_call(functools.partial(kernel, sizes), out_shape=(jax.ShapeDtyp...]
    unnamed x4 -> x2, local copies, waits for them, and re-layouts: 5.31 us -> 2.55 us
where the time goes in v2:
time: 97.9 us; the launch traced here: 97.6 us
  Pallas kernels  93.8 us (96%)
  local copies, waits for them, and re-layouts  2.55 us (3%)
  between operations  1.29 us (1%)
    pallas_call x1, Pallas kernels, local(): pl.pallas_call(functools.partial(kernel, sizes), out_shape=(jax.ShapeDtyp...  93.8 us
    unnamed x2, local copies, waits for them, and re-layouts  2.55 us

profile of v2, /device:TPU:1, one launch (start us, length us, event | category | flops | bytes accessed | tf_op | source)
XLA Modules:
  0.0 97.6 jit_solution(399925002809569433)
XLA Ops:
  1.3 93.8 %shard_map.140 = (f32[2,2,1024]{2,1,0:T(2,128)}, f32[2,2,18]{2,1,0:T(2,128)}) custom-call(s32[2,8]{1,0:T(2,128)} %bitcast.5, s32[8]{0:T(128)} %c_rows.1, s32[8]{0:T(128)} %c_side.1, s32[1]{0:T(128)S(6)} %copy.17.c_count, f32[2,2]{1,0:T(2,128)} %shifts.1, f32[2,2,32]{2,1,0:T(2,128)} %weights.1, f32[2,16,32]{2,1,0:T(8,128)} %bitcast.3, f32[2,32]{1,0:T(2,128)} %fresh.1, ...), custom_call_target="tpu_custom_call" | custom-call | tf_op jit(solution)/shard_map/pallas_call | solution.py:510
  95.0 1.3 %copy.18 = f32[2,2,1024]{2,1,0:T(2,128)} copy(f32[2,2,1024]{2,1,0:T(2,128)} %get-tuple-element.4) | data formatting | bytes 32768
  96.4 1.2 %copy.19 = f32[2,2,18]{2,1,0:T(2,128)} copy(f32[2,2,18]{2,1,0:T(2,128)} %get-tuple-element.5) | data formatting | bytes 576

commit v3 on v2

--- a/solution.py
+++ b/solution.py
@@ -39,12 +39,18 @@
     return lax.dot_general(a, b, NT_DIMS, preferred_element_type=F32)
 
 
-def own_columns(product, lanes):
-    lane = lax.broadcasted_iota(jnp.int32, (TILE, lanes), 1) % TD
-    total = jnp.zeros((TILE, lanes), F32)
+def in_two(matrix, start, stop, right):
+    half = TD // 2
+    parts = [nt(matrix[at * TILE : (at + half) * TILE, start:stop], right) for at in (0, half)]
+    return [parts[t // half][t % half * TILE : (t % half + 1) * TILE] for t in range(TD)]
+
+
+def own_columns(blocks):
+    lane = lax.broadcasted_iota(jnp.int32, blocks[0].shape, 1) % TD
+    totals = [jnp.zeros_like(blocks[0])] * 2
     for t in range(TD):
-        total = total + jnp.where(lane == t, product[t * TILE : (t + 1) * TILE], 0.0)
-    return total
+        totals[t // (TD // 2)] = jnp.where(lane == t, blocks[t], totals[t // (TD // 2)])
+    return totals[0] + totals[1]
 
 
 def fold(columns):
@@ -64,10 +70,10 @@
 
 def solve(entry):
     def g_re(a, b):
-        return entry(2 * a, UROW + 2 * b) + entry(2 * a + 1, UROW + 2 * b + 1)
+        return entry(2 * b, UROW + 2 * a) + entry(2 * b + 1, UROW + 2 * a + 1)
 
     def g_im(a, b):
-        return entry(2 * a, UROW + 2 * b + 1) - entry(2 * a + 1, UROW + 2 * b)
+        return entry(2 * b + 1, UROW + 2 * a) - entry(2 * b, UROW + 2 * a + 1)
 
     real, imag = {}, {}
     for a in range(ITERS):
@@ -177,9 +183,13 @@
     places = (sub, chip_y, chip_z * nc + core)
     stages = len(extents)
 
+    def order(stage):
+        chips, cores = extents[stage] // (nc if stage == 2 else 1), nc if stage == 2 else 1
+        return sorted(range(1, extents[stage]), key=lambda d: -min(d // cores, chips - d // cores))
+
     def send_sum(store, prefix, send_sem, recv_sem, stage):
         mine = store.at[(*prefix, stage, places[stage])]
-        for d in range(1, extents[stage]):
+        for d in order(stage):
             pltpu.make_async_remote_copy(
                 src_ref=mine,
                 dst_ref=mine,
@@ -327,8 +337,8 @@
         for it in range(ITERS):
             tiles = gathered[it]
             plain, turned = rows4(t_re, t_im), rows4(-t_im, t_re)
-            product = nt(p_two[...], jnp.concatenate([plain, plain, turned, turned], axis=1))
-            z_re, z_im = fold(own_columns(product, 32))
+            blocks = in_two(p_two, 0, 4 * TILE, jnp.concatenate([plain, plain, turned, turned], axis=1))
+            z_re, z_im = fold(own_columns(blocks))
             tiles[sub, 0] = z_re
             tiles[sub, 1] = z_im
             if it == 0:
@@ -347,7 +357,7 @@
                     device_id=who,
                     device_id_type=MESH,
                 ).start()
-            for d in range(1, ns):
+            for d in order(0):
                 pltpu.make_async_remote_copy(
                     src_ref=tiles.at[sub],
                     dst_ref=tiles.at[sub],
@@ -373,11 +383,15 @@
 
             to_stack(ZROW + 2 * it, z_re, z_im)
             own = rows4(z_re, z_im)
-            columns = own_columns(nt(k_two[:, 0 : 2 * TILE], jnp.concatenate([own, own], axis=1)), 32)
-            u_re, u_im = fold(columns)
+            blocks = in_two(k_two, 0, 2 * TILE, jnp.concatenate([own, own], axis=1))
+            u_re, u_im = fold(own_columns(blocks))
             moved_re, moved_im = mass[...] * z_re, mass[...] * z_im
             u_re = u_re - (shift_re * moved_re - shift_im * moved_im)
             u_im = u_im - (shift_re * moved_im + shift_im * moved_re)
+
+            if it == ITERS - 1:
+                both = gram(stack[PREV : RIGHT + 2, :], stack[0:XROWS, :])
+                packed = jnp.where(lane < UROW, both[0:8], jnp.where(lane < RIGHT + 2, both[8:16], 0.0))
 
             wait_for(halo.at[turn], halo_recv.at[turn])
             sides = []
@@ -386,10 +400,10 @@
                 im = jnp.broadcast_to(halo[turn, side, 1, tile : tile + 1, :], (8, TILE))
                 sides.append(rows4(re, im))
             rims = jnp.concatenate(sides, axis=0)
-            product = nt(c_two[...], jnp.concatenate([rims, rims], axis=1))
+            blocks = in_two(c_two, 0, 2 * TILE, jnp.concatenate([rims, rims], axis=1))
             columns = jnp.zeros((TILE, 64), F32)
             for j in range(TD):
-                columns = columns + slot_masks[j : j + 1, :] * product[j * TILE : (j + 1) * TILE]
+                columns = columns + slot_masks[j : j + 1, :] * blocks[j]
             c_re, c_im = fold(columns)
             u_re, u_im = u_re + c_re, u_im + c_im
 
@@ -401,16 +415,25 @@
                         picked[q, c, t : t + 1, :] = tiles[source // TD, c, pl.ds(source % TD, 1), :]
             first = rows4(picked[0, 0], picked[0, 1])
             second = rows4(picked[1, 0], picked[1, 1])
-            product = nt(k_two[:, 2 * TILE :], jnp.concatenate([first, first, second, second], axis=1))
-            k_re, k_im = fold(own_columns(product, 32))
+            blocks = in_two(k_two, 2 * TILE, 6 * TILE, jnp.concatenate([first, first, second, second], axis=1))
+            k_re, k_im = fold(own_columns(blocks))
             u_re, u_im = u_re + k_re, u_im + k_im
             to_stack(UROW + 2 * it, u_re, u_im)
             t_re, t_im = u_re - t_re, u_im - t_im
+            if it == ITERS - 1:
+                with_u_re = jnp.zeros((8, TILE), F32)
+                with_u_im = jnp.zeros((8, TILE), F32)
+                for t in range(TD):
+                    block = stack[UROW : RIGHT + 2, t * TILE : (t + 1) * TILE]
+                    with_u_re = with_u_re + block * u_re[t : t + 1]
+                    with_u_im = with_u_im + block * u_im[t : t + 1]
+                with_u_re = jnp.sum(with_u_re, axis=1, keepdims=True)
+                with_u_im = jnp.sum(with_u_im, axis=1, keepdims=True)
+                last = UROW + 2 * it
+                packed = jnp.where(lane == last, with_u_re, jnp.where(lane == last + 1, with_u_im, packed))
             wait_for(halo.at[turn], halo_send.at[turn])
             wait_for(tiles.at[pl.ds(0, ns - 1)], tile_send.at[turn])
 
-        both = gram(stack[PREV:48, :], stack[0:XROWS, :])
-        packed = jnp.where(lane < UROW, both[0:8], jnp.where(lane < RIGHT + 2, both[8:16], 0.0))
         part = packed[0:4] + pltpu.roll(packed[4:8], 64, 1)
         for stage in range(stages):
             sums[step, stage, places[stage]] = part
@@ -495,6 +518,11 @@
         one_step(step)
 
 
+def hand_over(made, listed, made_out, listed_out):
+    made_out[...] = made[...]
+    listed_out[...] = listed[...]
+
+
 def solution(mesh, y_chips=None):
     ns, n_dom = mesh.shape["sub"], mesh.shape["dom"]
     nz = Z_CHIPS if y_chips is None else n_dom // CORES // y_chips
@@ -507,7 +535,7 @@
         anywhere = pl.BlockSpec(memory_space=pl.ANY)
         steps = weights.shape[0]
         rows = TD * TILE
-        return pl.pallas_call(
+        made, listed = pl.pallas_call(
             functools.partial(kernel, sizes),
             out_shape=(
                 jax.ShapeDtypeStruct((steps, 2, rows), F32),
@@ -561,6 +589,15 @@
             precond,
             c_tiles,
         )
+        return pl.pallas_call(
+            hand_over,
+            out_shape=(
+                jax.ShapeDtypeStruct((steps, 2, rows), F32),
+                jax.ShapeDtypeStruct((steps, 2, NB + 2), F32),
+            ),
+            in_specs=[vmem] * 2,
+            out_specs=(vmem, vmem),
+        )(made, listed)
 
     both = ("dom", "sub")
     placed = (

time: 97.9 us -> 90.5 us (0.924)
  Pallas kernels: 93.8 us -> 89 us
  local copies, waits for them, and re-layouts: 2.55 us -> 0 us
    pallas_call x1, Pallas kernels: 93.8 us -> 87.6 us  [local(): pl.pallas_call(functools.partial(kernel, sizes), out_shape=(jax.ShapeDtyp...]
    unnamed x2 -> x0, local copies, waits for them, and re-layouts: 2.55 us -> none
    pallas_call x0 -> x1, Pallas kernels: none -> 1.33 us  [local(): pl.pallas_call(hand_over, out_shape=(jax.ShapeDtypeStruct((steps, 2, rows...]
where the time goes in v3:
time: 90.5 us; the launch traced here: 90.3 us
  Pallas kernels  89 us (98%)
  between operations  1.29 us (1%)
    pallas_call x1, Pallas kernels, local(): pl.pallas_call(functools.partial(kernel, sizes), out_shape=(jax.ShapeDtyp...  87.6 us

profile of v3, /device:TPU:1, one launch (start us, length us, event | category | flops | bytes accessed | tf_op | source)
XLA Modules:
  0.0 90.3 jit_solution(12709969695771531868)
XLA Ops:
  1.3 87.6 %shard_map.140 = (f32[2,2,1024]{2,1,0:T(2,128)}, f32[2,2,18]{2,1,0:T(2,128)}) custom-call(s32[2,8]{1,0:T(2,128)} %bitcast.5, s32[8]{0:T(128)} %c_rows.1, s32[8]{0:T(128)} %c_side.1, s32[1]{0:T(128)S(6)} %copy.15.c_count, f32[2,2]{1,0:T(2,128)} %shifts.1, f32[2,2,32]{2,1,0:T(2,128)} %weights.1, f32[2,16,32]{2,1,0:T(8,128)} %bitcast.3, f32[2,32]{1,0:T(2,128)} %fresh.1, ...), custom_call_target="tpu_custom_call" | custom-call | tf_op jit(solution)/shard_map/pallas_call | solution.py:538
  88.9 1.3 %shard_map.141 = (f32[2,2,1024]{2,1,0:T(2,128)}, f32[2,2,18]{2,1,0:T(2,128)}) custom-call(f32[2,2,1024]{2,1,0:T(2,128)} %get-tuple-element.4.made, f32[2,2,18]{2,1,0:T(2,128)} %get-tuple-element.5.listed), custom_call_target="tpu_custom_call" | custom-call | tf_op jit(solution)/shard_map/pallas_call | solution.py:592

commit v4 on v3

--- a/solution.py
+++ b/solution.py
@@ -118,15 +118,15 @@
 
 def kernel(
     sizes,
-    pattern,
-    c_rows,
-    c_side,
+    pattern_hbm,
+    c_rows_hbm,
+    c_side_hbm,
     c_count,
-    shifts,
-    weights,
-    compact,
-    fresh,
-    mass,
+    shifts_hbm,
+    weights_hbm,
+    compact_hbm,
+    fresh_hbm,
+    mass_hbm,
     basis,
     k_hbm,
     p_hbm,
@@ -152,6 +152,14 @@
     sums,
     basis_sums,
     slot_masks,
+    pattern,
+    c_rows,
+    c_side,
+    shifts,
+    weights,
+    compact,
+    fresh,
+    mass,
     load_sem,
     tile_send,
     tile_recv,
@@ -212,20 +220,29 @@
         return total
     lower_dom, upper_dom = ((dom + n_dom - 1) % n_dom, sub), ((dom + 1) % n_dom, sub)
 
-    loads = [
-        pltpu.make_async_copy(basis.at[0], stack.at[pl.ds(0, NB)], load_sem.at[0]),
-        pltpu.make_async_copy(basis.at[1], stack.at[pl.ds(NB, NB)], load_sem.at[1]),
-        pltpu.make_async_copy(p_hbm, p_raw, load_sem.at[2]),
-        pltpu.make_async_copy(k_hbm, k_raw, load_sem.at[3]),
-        pltpu.make_async_copy(c_hbm, c_raw, load_sem.at[4]),
-    ]
+    pairs = (
+        (weights_hbm, weights),
+        (compact_hbm, compact),
+        (fresh_hbm, fresh),
+        (basis.at[0], stack.at[pl.ds(0, NB)]),
+        (basis.at[1], stack.at[pl.ds(NB, NB)]),
+        (p_hbm, p_raw),
+        (shifts_hbm, shifts),
+        (mass_hbm, mass),
+        (pattern_hbm, pattern),
+        (c_rows_hbm, c_rows),
+        (c_side_hbm, c_side),
+        (k_hbm, k_raw),
+        (c_hbm, c_raw),
+    )
+    loads = [pltpu.make_async_copy(source, target, load_sem.at[n]) for n, (source, target) in enumerate(pairs)]
     for load in loads:
         load.start()
 
     barrier = pltpu.get_barrier_semaphore()
     greeted = 0
     for stage in range(stages):
-        for d in range(1, extents[stage]):
+        for d in order(stage):
             pl.semaphore_signal(barrier, inc=1, device_id=along(stage, d), device_id_type=MESH)
             greeted += 1
     for who in (lower_dom, upper_dom):
@@ -235,6 +252,9 @@
     lane = lax.broadcasted_iota(jnp.int32, (8, TILE), 1)
     row = lax.broadcasted_iota(jnp.int32, (8, TILE), 0)
     lane2 = lax.broadcasted_iota(jnp.int32, (NB, TILE), 1)
+
+    for load in loads[0:3]:
+        load.wait()
 
     terms = weights.shape[2]
     coef_table[...] = jnp.zeros_like(coef_table)
@@ -266,10 +286,8 @@
         right_coef[k, 1:2, :] = second
 
     stack[pl.ds(PREV, 16), :] = jnp.zeros((16, TD * TILE), F32)
-    loads[0].wait()
-    loads[1].wait()
-
-    loads[2].wait()
+    for load in loads[3:6]:
+        load.wait()
 
     @pl.loop(0, TD)
     def _(t):
@@ -278,6 +296,8 @@
             p_two[pl.ds(t * TILE, TILE), (2 * c) * TILE : (2 * c + 1) * TILE] = hi
             p_two[pl.ds(t * TILE, TILE), (2 * c + 1) * TILE : (2 * c + 2) * TILE] = lo
 
+    for load in loads[6:11]:
+        load.wait()
     gathered = (tiles0, tiles1, tiles2)
 
     def late_start():
@@ -304,7 +324,7 @@
         send_sum(basis_sums, (), basis_send, basis_recv, 0)
 
     def split_rest():
-        loads[3].wait()
+        loads[11].wait()
 
         @pl.loop(0, TD)
         def _(t):
@@ -313,7 +333,7 @@
                 k_two[pl.ds(t * TILE, TILE), (2 * q) * TILE : (2 * q + 1) * TILE] = hi
                 k_two[pl.ds(t * TILE, TILE), (2 * q + 1) * TILE : (2 * q + 2) * TILE] = lo
 
-        loads[4].wait()
+        loads[12].wait()
 
         @pl.loop(0, TD)
         def _(t):
@@ -530,7 +550,6 @@
     most = max(ns, sizes[0], nz * CORES)
 
     def local(basis, compact, weights, fresh, shifts, k_tiles, pattern, mass, precond, c_tiles, c_rows, c_side, c_count):
-        smem = pl.BlockSpec(memory_space=pltpu.SMEM)
         vmem = pl.BlockSpec(memory_space=pltpu.VMEM)
         anywhere = pl.BlockSpec(memory_space=pl.ANY)
         steps = weights.shape[0]
@@ -541,7 +560,7 @@
                 jax.ShapeDtypeStruct((steps, 2, rows), F32),
                 jax.ShapeDtypeStruct((steps, 2, NB + 2), F32),
             ),
-            in_specs=[smem] * 5 + [vmem] * 4 + [anywhere] * 4,
+            in_specs=[anywhere] * 3 + [pl.BlockSpec(memory_space=pltpu.SMEM)] + [anywhere] * 9,
             out_specs=(vmem, vmem),
             scratch_shapes=[
                 pltpu.VMEM((TD, 3, TILE, TILE), F32),
@@ -563,7 +582,15 @@
                 pltpu.VMEM((steps, 3, most, 4, TILE), F32),
                 pltpu.VMEM((3, most, 4, TILE), F32),
                 pltpu.VMEM((TD, 64), F32),
-                pltpu.SemaphoreType.DMA((5,)),
+                pltpu.SMEM((2, TD), jnp.int32),
+                pltpu.SMEM((TD,), jnp.int32),
+                pltpu.SMEM((TD,), jnp.int32),
+                pltpu.SMEM((steps, 2), F32),
+                pltpu.VMEM(weights.shape, F32),
+                pltpu.VMEM((2, NB, weights.shape[2]), F32),
+                pltpu.VMEM(fresh.shape, F32),
+                pltpu.VMEM((TD, TILE), F32),
+                pltpu.SemaphoreType.DMA((13,)),
                 pltpu.SemaphoreType.DMA((steps * ITERS,)),
                 pltpu.SemaphoreType.DMA((steps * ITERS,)),
                 pltpu.SemaphoreType.DMA((steps * ITERS,)),

time: 90.5 us -> 89.7 us (level)
  no operation moved by 1% of the time
where the time goes in v4:
time: 89.7 us; the launch traced here: 89.4 us
  Pallas kernels  88.1 us (98%)
  between operations  1.29 us (1%)
    pallas_call x1, Pallas kernels, local(): pl.pallas_call(functools.partial(kernel, sizes), out_shape=(jax.ShapeDtyp...  86.8 us

profile of v4, /device:TPU:1, one launch (start us, length us, event | category | flops | bytes accessed | tf_op | source)
XLA Modules:
  0.0 89.4 jit_solution(1874486291981586335)
XLA Ops:
  1.3 86.8 %shard_map.140 = (f32[2,2,1024]{2,1,0:T(2,128)}, f32[2,2,18]{2,1,0:T(2,128)}) custom-call(s32[2,8]{1,0:T(2,128)} %bitcast.5, s32[8]{0:T(128)} %c_rows_hbm.1, s32[8]{0:T(128)} %c_side_hbm.1, s32[1]{0:T(128)S(6)} %copy.15.c_count, f32[2,2]{1,0:T(2,128)} %shifts_hbm.1, f32[2,2,32]{2,1,0:T(2,128)} %weights_hbm.1, f32[2,16,32]{2,1,0:T(8,128)} %bitcast.3, ...), custom_call_target="tpu_custom_call" | custom-call | tf_op jit(solution)/shard_map/pallas_call | solution.py:557
  88.1 1.3 %shard_map.141 = (f32[2,2,1024]{2,1,0:T(2,128)}, f32[2,2,18]{2,1,0:T(2,128)}) custom-call(f32[2,2,1024]{2,1,0:T(2,128)} %get-tuple-element.4.made, f32[2,2,18]{2,1,0:T(2,128)} %get-tuple-element.5.listed), custom_call_target="tpu_custom_call" | custom-call | tf_op jit(solution)/shard_map/pallas_call | solution.py:619
